TPU v7x, 128 devices: a whole 4x4x4 slice. The times are simulated.
128 devices in a mesh: strip: 32 (over y, x, core), sub: 4 (over z).
Axes of the slice: x: 4, y: 4, z: 4, core: 2. Of those that a mesh axis runs over, the one named last changes fastest.
Arguments:
- counts: int32 [1024, 32768], P('strip', 'sub'), may hold values from 0 to 5
- offset: float32 [1024, 32768], P('strip', 'sub'), may hold values from -1.2 to 1.45
- kappa: float32 [1024, 32768], P('strip', 'sub'), may hold values from 0.01 to 1
- labels: int32 [8, 256], P(None, 'sub'), may hold values from 0 to 1023
- owner: int32 [1024], replicated, may hold values from 0 to 127, as said below
Outputs:
- mode: float32 [1024, 32768], P('strip', 'sub')
- owned: float32 [1920], P(('strip', 'sub'))
Inputs may be any that keep to these rules, and one draw needn't show every extreme that they name: owner of each region as an index along strip+sub (strip slowest); each device owns 1 to 15 regions, and some device exactly 15.
All inputs are finite; a program needn't handle non-finite values.
Results may differ from a plain program's by a relative error of at most 0.0001.
Values sent between devices are 32-bit elements; how exact they have to be, the bound alone decides.
A program may use at most 64 MiB of HBM per device.

v0:
```python
import functools

import jax
import jax.numpy as jnp
from jax import lax
from jax.sharding import Mesh
from jax.sharding import PartitionSpec as P

TILE = 128
NEWTON_STEPS = 2
INNER_STEPS = 3
OWNED_MOST = 15
STRIP_SUB = ("strip_0", "strip_1", "strip_2", "sub")
STRIP = ("strip_0", "strip_1", "strip_2")


prior_scale = 0.1


def padded_2(block, sides, width):
    for axis, dim in sides:
        count = lax.axis_size(axis)
        forward = [(i, i + 1) for i in range(count - 1)]
        backward = [(target, source) for source, target in forward]
        low = lax.ppermute(
            lax.slice_in_dim(block, block.shape[dim] - width, None, axis=dim), axis, forward
        )
        high = lax.ppermute(lax.slice_in_dim(block, 0, width, axis=dim), axis, backward)
        block = jnp.concatenate([low, block, high], axis=dim)
    return block


def one_axis_at_a_time(array, axes):
    return functools.reduce(lax.psum, axes, array)


def extended(array, sides, width):
    edges = {}
    for axis, dim in sides:
        devices, length = (lax.axis_size(axis), array.shape[dim])
        up = [(i, (i + 1) % devices) for i in range(devices - 1)]
        last = lax.slice_in_dim(array, length - width, length, axis=dim)
        initial = lax.slice_in_dim(array, 0, width, axis=dim)
        edges[dim] = (
            lax.ppermute(last, axis, up),
            lax.ppermute(initial, axis, [(b, a) for a, b in up]),
        )
    done = []
    for _, dim in sides:
        low, high = edges[dim]
        around = [(width, width) if d in done else (0, 0) for d in range(array.ndim)]
        array = jnp.concatenate([jnp.pad(low, around), array, jnp.pad(high, around)], axis=dim)
        done.append(dim)
    return array


def neighbours(padded):
    return padded[2:, 1:-1] + padded[:-2, 1:-1] + padded[1:-1, 2:] + padded[1:-1, :-2]


def wide_apply(field, kappa, kappa_wide, inside):
    padded = padded_2(field, ((STRIP, 0), ("sub", 1)), 2)
    first = ((kappa_wide + 4.0) * padded[1:-1, 1:-1] - neighbours(padded)) * inside
    return prior_scale * ((kappa + 4.0) * first[1:-1, 1:-1] - neighbours(first))


def paired(residual, image):
    return (
        one_axis_at_a_time(jnp.sum(residual * residual), STRIP_SUB),
        one_axis_at_a_time(jnp.sum(residual * image), STRIP_SUB),
    )


def joined_solve(gradient, weight, operator):
    step = jnp.zeros_like(gradient)
    residual = gradient
    image = operator(residual) + weight * residual
    norm_now, product = paired(residual, image)
    alpha = norm_now / product
    direction = residual
    along = image
    for inner_step in range(INNER_STEPS):
        step = step + alpha * direction
        residual = residual - alpha * along
        if inner_step + 1 < INNER_STEPS:
            image = operator(residual) + weight * residual
            norm_next, product = paired(residual, image)
            ratio = norm_next / norm_now
            alpha = norm_next / (product - ratio * norm_next / alpha)
            direction = residual + ratio * direction
            along = image + ratio * along
            norm_now = norm_next
    return step


def body(counts, offset, kappa, labels, owner):
    height, width = offset.shape
    kappa_wide = extended(kappa, ((STRIP, 0), ("sub", 1)), 1)
    row_ids = jnp.arange(height + 2, dtype=jnp.int32) - 1 + lax.axis_index(STRIP) * height
    col_ids = jnp.arange(width + 2, dtype=jnp.int32) - 1 + lax.axis_index("sub") * width
    row_fine = (row_ids >= 0) & (row_ids < height * lax.axis_size(STRIP))
    col_fine = (col_ids >= 0) & (col_ids < width * lax.axis_size("sub"))
    inside = (row_fine[:, None] & col_fine[None, :]).astype(jnp.float32)

    def operator(field):
        return wide_apply(field, kappa, kappa_wide, inside)

    observed = counts.astype(jnp.float32)
    mode = jnp.zeros(offset.shape, jnp.float32)
    for newton_step in range(NEWTON_STEPS):
        weight = jnp.exp(offset + mode)
        gradient = observed - weight - operator(mode)
        step = joined_solve(gradient, weight, operator)
        mode = mode + step
    intensity = jnp.exp(offset + mode)
    span = min(height, TILE)
    tile_rows = height // span
    tile_sums = intensity.reshape(tile_rows, span, width // TILE, TILE).sum(axis=(1, 3)) / float(
        TILE * TILE
    )
    first_row = lax.axis_index(STRIP) * height // TILE
    label_block = lax.dynamic_slice_in_dim(labels, first_row, tile_rows, 0)
    regions = owner.shape[0]
    devices = lax.axis_size(STRIP) * lax.axis_size("sub")
    local = jax.ops.segment_sum(
        tile_sums.reshape(-1), label_block.reshape(-1), num_segments=regions
    )
    marks = (owner[:, None] == jnp.arange(devices, dtype=jnp.int32)[None, :]).astype(jnp.int32)
    slots = jnp.sum((jnp.cumsum(marks, axis=0) - marks) * marks, axis=1)
    myself = lax.axis_index(STRIP) * lax.axis_size("sub") + lax.axis_index("sub")
    totals = one_axis_at_a_time(local, STRIP_SUB)
    owned = jax.ops.segment_sum(
        jnp.where(owner == myself, totals, 0.0), slots, num_segments=OWNED_MOST
    )
    return (mode, owned)


def solution(mesh):
    finer = Mesh(
        mesh.devices.reshape(4, 4, 2, mesh.shape["sub"]), ("strip_0", "strip_1", "strip_2", "sub")
    )
    return jax.shard_map(
        body,
        mesh=finer,
        in_specs=(P(STRIP, "sub"), P(STRIP, "sub"), P(STRIP, "sub"), P(None, "sub"), P()),
        out_specs=(P(STRIP, "sub"), P(STRIP_SUB)),
        check_vma=False,
    )
```

profile of v0, /device:TPU:0, one launch (start us, length us, event | category | flops | bytes accessed | tf_op | source)
XLA Modules:
  0.0 506.7 jit_solution(8082975455588305184)
XLA Ops:
  5.0 5.5 %collective-permute-start.1 = (f32[1,8192]{1,0:T(1,128)}, f32[1,8192]{1,0:T(1,128)}, u32[]{:S(2)}, u32[]{:S(2)}) collective-permute-start(f32[1,8192]{1,0:T(1,128)} %get-tuple-element.102), channel_id=1, source_target_pairs={{0,4},{4,8},{8,12},{12,16},{16,20},{20,24},{24,28},{28,32},{32,36}... | collective-permute-start | bytes 98312 | tf_op jit(solution)/shard_map/ppermute | solution.py:45
  11.2 3.8 collective-permute-start
  23.4 3.8 collective-permute-start.6
  33.1 2.5 concatenate.105
  35.6 4.1 and_select_fusion.7
  43.6 3.4 collective-permute-done.9
  48.3 3.9 collective-permute-start.10
  53.7 4.2 collective-permute-done.11
  60.4 4.1 and_select_fusion.6
  64.6 2.7 multiply_reduce_fusion.8
  67.3 19.0 %all-reduce.19 = (f32[]{:T(128)}, f32[]{:T(128)}) all-reduce(f32[]{:T(128)} %get-tuple-element.13, f32[]{:T(128)} %get-tuple-element.12), channel_id=1, replica_groups=mesh['strip_0'=4,'strip_1'=4,'strip_2'=2,'sub'=4] {'strip_0'}, use_global_device_ids=true, to_apply=%region_1.2 | all-reduce | flops 2 | bytes 16 | tf_op jit(solution)/shard_map/psum | solution.py:34
  86.3 8.3 %all-reduce.13 = (f32[]{:T(128)}, f32[]{:T(128)}) all-reduce(f32[]{:T(128)} %get-tuple-element.48, f32[]{:T(128)} %get-tuple-element.49), channel_id=1, replica_groups=mesh['strip_0'=4,'strip_1'=4,'strip_2'=2,'sub'=4] {'strip_1'}, use_global_device_ids=true, to_apply=%region_2.3 | all-reduce | flops 2 | bytes 16 | tf_op jit(solution)/shard_map/psum | solution.py:34
  94.7 3.2 all-reduce.25
  97.8 10.1 %all-reduce.7 = (f32[]{:T(128)}, f32[]{:T(128)}) all-reduce(f32[]{:T(128)} %get-tuple-element.60, f32[]{:T(128)} %get-tuple-element.61), channel_id=1, replica_groups=mesh['strip_0'=4,'strip_1'=4,'strip_2'=2,'sub'=4] {'sub'}, use_global_device_ids=true, to_apply=%region_4.5 | all-reduce | flops 2 | bytes 16 | tf_op jit(solution)/shard_map/psum | solution.py:34
  113.3 4.1 collective-permute-done.13
  118.6 2.9 collective-permute-start.14
  123.0 4.2 collective-permute-done.15
  129.7 4.7 and_select_fusion.5
  134.5 2.8 multiply_reduce_fusion.6
  137.3 11.0 %all-reduce.18 = (f32[]{:T(128)}, f32[]{:T(128)}) all-reduce(f32[]{:T(128)} %get-tuple-element.11, f32[]{:T(128)} %get-tuple-element.10), channel_id=1, replica_groups=mesh['strip_0'=4,'strip_1'=4,'strip_2'=2,'sub'=4] {'strip_0'}, use_global_device_ids=true, to_apply=%region_11.12 | all-reduce | flops 2 | bytes 16 | tf_op jit(solution)/shard_map/psum | solution.py:34
  148.4 8.6 %all-reduce.12 = (f32[]{:T(128)}, f32[]{:T(128)}) all-reduce(f32[]{:T(128)} %get-tuple-element.46, f32[]{:T(128)} %get-tuple-element.47), channel_id=1, replica_groups=mesh['strip_0'=4,'strip_1'=4,'strip_2'=2,'sub'=4] {'strip_1'}, use_global_device_ids=true, to_apply=%region_12.13 | all-reduce | flops 2 | bytes 16 | tf_op jit(solution)/shard_map/psum | solution.py:34
  157.0 3.1 all-reduce.24
  160.1 8.4 %all-reduce.6 = (f32[]{:T(128)}, f32[]{:T(128)}) all-reduce(f32[]{:T(128)} %get-tuple-element.58, f32[]{:T(128)} %get-tuple-element.59), channel_id=1, replica_groups=mesh['strip_0'=4,'strip_1'=4,'strip_2'=2,'sub'=4] {'sub'}, use_global_device_ids=true, to_apply=%region_14.15 | all-reduce | flops 2 | bytes 16 | tf_op jit(solution)/shard_map/psum | solution.py:34
  177.4 3.9 collective-permute-done.17
  182.6 3.9 collective-permute-start.18
  187.9 4.2 collective-permute-done.19
  194.7 4.8 and_select_fusion.4
  201.3 13.5 %all-reduce.17 = (f32[]{:T(128)}, f32[]{:T(128)}) all-reduce(f32[]{:T(128)} %get-tuple-element.9, f32[]{:T(128)} %get-tuple-element.8), channel_id=1, replica_groups=mesh['strip_0'=4,'strip_1'=4,'strip_2'=2,'sub'=4] {'strip_0'}, use_global_device_ids=true, to_apply=%region_21.22 | all-reduce | flops 2 | bytes 16 | tf_op jit(solution)/shard_map/psum | solution.py:34
  214.8 8.4 %all-reduce.11 = (f32[]{:T(128)}, f32[]{:T(128)}) all-reduce(f32[]{:T(128)} %get-tuple-element.44, f32[]{:T(128)} %get-tuple-element.45), channel_id=1, replica_groups=mesh['strip_0'=4,'strip_1'=4,'strip_2'=2,'sub'=4] {'strip_1'}, use_global_device_ids=true, to_apply=%region_22.23 | all-reduce | flops 2 | bytes 16 | tf_op jit(solution)/shard_map/psum | solution.py:34
  223.1 3.1 all-reduce.23
  226.3 8.4 %all-reduce.5 = (f32[]{:T(128)}, f32[]{:T(128)}) all-reduce(f32[]{:T(128)} %get-tuple-element.56, f32[]{:T(128)} %get-tuple-element.57), channel_id=1, replica_groups=mesh['strip_0'=4,'strip_1'=4,'strip_2'=2,'sub'=4] {'sub'}, use_global_device_ids=true, to_apply=%region_24.25 | all-reduce | flops 2 | bytes 16 | tf_op jit(solution)/shard_map/psum | solution.py:34
  243.0 4.1 collective-permute-done.21
  247.3 3.9 collective-permute-start.22
  252.9 4.2 collective-permute-done.23
  259.6 4.1 and_select_fusion.3
  266.7 3.4 collective-permute-start.24
  280.9 3.4 collective-permute-done.27
  286.8 4.1 and_select_fusion.2
  290.9 2.9 multiply_reduce_fusion.3
  293.8 13.1 %all-reduce.16 = (f32[]{:T(128)}, f32[]{:T(128)}) all-reduce(f32[]{:T(128)} %get-tuple-element.7, f32[]{:T(128)} %get-tuple-element.6), channel_id=1, replica_groups=mesh['strip_0'=4,'strip_1'=4,'strip_2'=2,'sub'=4] {'strip_0'}, use_global_device_ids=true, to_apply=%region_31.32 | all-reduce | flops 2 | bytes 16 | tf_op jit(solution)/shard_map/psum | solution.py:34
  306.9 8.4 %all-reduce.10 = (f32[]{:T(128)}, f32[]{:T(128)}) all-reduce(f32[]{:T(128)} %get-tuple-element.42, f32[]{:T(128)} %get-tuple-element.43), channel_id=1, replica_groups=mesh['strip_0'=4,'strip_1'=4,'strip_2'=2,'sub'=4] {'strip_1'}, use_global_device_ids=true, to_apply=%region_32.33 | all-reduce | flops 2 | bytes 16 | tf_op jit(solution)/shard_map/psum | solution.py:34
  315.3 3.1 all-reduce.22
  318.4 9.8 %all-reduce.4 = (f32[]{:T(128)}, f32[]{:T(128)}) all-reduce(f32[]{:T(128)} %get-tuple-element.54, f32[]{:T(128)} %get-tuple-element.55), channel_id=1, replica_groups=mesh['strip_0'=4,'strip_1'=4,'strip_2'=2,'sub'=4] {'sub'}, use_global_device_ids=true, to_apply=%region_34.35 | all-reduce | flops 2 | bytes 16 | tf_op jit(solution)/shard_map/psum | solution.py:34
  335.1 3.7 collective-permute-done.29
  345.7 3.4 collective-permute-done.31
  351.7 4.1 and_select_fusion.1
  355.8 2.8 multiply_reduce_fusion.1
  358.6 11.7 %all-reduce.15 = (f32[]{:T(128)}, f32[]{:T(128)}) all-reduce(f32[]{:T(128)} %get-tuple-element.5, f32[]{:T(128)} %get-tuple-element.4), channel_id=1, replica_groups=mesh['strip_0'=4,'strip_1'=4,'strip_2'=2,'sub'=4] {'strip_0'}, use_global_device_ids=true, to_apply=%region_41.42 | all-reduce | flops 2 | bytes 16 | tf_op jit(solution)/shard_map/psum | solution.py:34
  370.3 8.4 %all-reduce.9 = (f32[]{:T(128)}, f32[]{:T(128)}) all-reduce(f32[]{:T(128)} %get-tuple-element.40, f32[]{:T(128)} %get-tuple-element.41), channel_id=1, replica_groups=mesh['strip_0'=4,'strip_1'=4,'strip_2'=2,'sub'=4] {'strip_1'}, use_global_device_ids=true, to_apply=%region_42.43 | all-reduce | flops 2 | bytes 16 | tf_op jit(solution)/shard_map/psum | solution.py:34
  378.7 3.2 all-reduce.21
  381.9 8.8 %all-reduce.3 = (f32[]{:T(128)}, f32[]{:T(128)}) all-reduce(f32[]{:T(128)} %get-tuple-element.52, f32[]{:T(128)} %get-tuple-element.53), channel_id=1, replica_groups=mesh['strip_0'=4,'strip_1'=4,'strip_2'=2,'sub'=4] {'sub'}, use_global_device_ids=true, to_apply=%region_44.45 | all-reduce | flops 2 | bytes 16 | tf_op jit(solution)/shard_map/psum | solution.py:34
  402.2 3.5 collective-permute-done.33
  408.9 3.7 collective-permute-start.34
  414.4 4.1 collective-permute-done.35
  421.0 4.6 and_select_fusion
  427.4 12.7 %all-reduce.14 = (f32[]{:T(128)}, f32[]{:T(128)}) all-reduce(f32[]{:T(128)} %get-tuple-element.3, f32[]{:T(128)} %get-tuple-element.2), channel_id=1, replica_groups=mesh['strip_0'=4,'strip_1'=4,'strip_2'=2,'sub'=4] {'strip_0'}, use_global_device_ids=true, to_apply=%region_51.52 | all-reduce | flops 2 | bytes 16 | tf_op jit(solution)/shard_map/psum | solution.py:34
  440.1 8.3 %all-reduce.8 = (f32[]{:T(128)}, f32[]{:T(128)}) all-reduce(f32[]{:T(128)} %get-tuple-element.38, f32[]{:T(128)} %get-tuple-element.39), channel_id=1, replica_groups=mesh['strip_0'=4,'strip_1'=4,'strip_2'=2,'sub'=4] {'strip_1'}, use_global_device_ids=true, to_apply=%region_52.53 | all-reduce | flops 2 | bytes 16 | tf_op jit(solution)/shard_map/psum | solution.py:34
  448.5 3.1 all-reduce.20
  451.6 8.4 %all-reduce.2 = (f32[]{:T(128)}, f32[]{:T(128)}) all-reduce(f32[]{:T(128)} %get-tuple-element.50, f32[]{:T(128)} %get-tuple-element.51), channel_id=1, replica_groups=mesh['strip_0'=4,'strip_1'=4,'strip_2'=2,'sub'=4] {'sub'}, use_global_device_ids=true, to_apply=%region_54.55 | all-reduce | flops 2 | bytes 16 | tf_op jit(solution)/shard_map/psum | solution.py:34
  463.7 3.4 exponential_reduce_fusion
  468.4 8.2 %psum.412 = f32[1024]{0:T(1024)S(1)} all-reduce(f32[1024]{0:T(1024)S(1)} %scatter_custom_fusion), channel_id=1, replica_groups=mesh['strip_0'=4,'strip_1'=4,'strip_2'=2,'sub'=4] {'strip_0'}, use_global_device_ids=true, to_apply=%region_66.67 | all-reduce | flops 1024 | bytes 8192 | tf_op jit(solution)/shard_map/psum | solution.py:34
  476.6 9.3 %psum.413 = f32[1024]{0:T(1024)S(1)} all-reduce(f32[1024]{0:T(1024)S(1)} %psum.412), channel_id=1, replica_groups=mesh['strip_0'=4,'strip_1'=4,'strip_2'=2,'sub'=4] {'strip_1'}, use_global_device_ids=true, to_apply=%region_67.68 | all-reduce | flops 1024 | bytes 8192 | tf_op jit(solution)/shard_map/psum | solution.py:34
  488.3 9.7 %psum.415 = f32[1024]{0:T(1024)S(1)} all-reduce(f32[1024]{0:T(1024)S(1)} %psum.414), channel_id=1, replica_groups=mesh['strip_0'=4,'strip_1'=4,'strip_2'=2,'sub'=4] {'sub'}, use_global_device_ids=true, to_apply=%region_69.70 | all-reduce | flops 1024 | bytes 8192 | tf_op jit(solution)/shard_map/psum | solution.py:34
  498.0 8.3 %scatter_custom_fusion.1 = f32[15]{0:T(128)} fusion(s32[1024]{0:T(1024)} %fusion.53, f32[1024]{0:T(1024)S(1)} %compare_select_fusion, f32[]{:T(128)} %constant.73.clone.1), kind=kCustom, calls=%fused_computation.206 | custom fusion | flops 1024 | bytes 572 | tf_op jit(solution)/shard_map/scatter-add | solution.py:132
  (193 shorter events, 109.6 us)
Async XLA Ops:
  0.6 413.2 %copy-start = (s32[8,64]{1,0:T(8,128)S(1)}, s32[8,64]{1,0:T(8,128)}, u32[]{:S(2)}) copy-start(s32[8,64]{1,0:T(8,128)} %param.8) | copy-start | bytes 6148
  0.7 20.7 %collective-permute-start.4 = (f32[2,8192]{1,0:T(2,128)S(1)}, f32[2,8192]{1,0:T(2,128)S(1)}, u32[]{:S(2)}, u32[]{:S(2)}) collective-permute-start(f32[2,8192]{1,0:T(2,128)S(1)} %broadcast.91), channel_id=1, source_target_pairs={{0,4},{4,8},{8,12},{12,16},{16,20},{20,24},{24,28},{28,32},{32,36}... | collective-permute-start | bytes 196616 | tf_op jit(solution)/shard_map/ppermute | solution.py:25
  2.0 19.4 %collective-permute-start.5 = (f32[2,8192]{1,0:T(2,128)S(1)}, f32[2,8192]{1,0:T(2,128)}, u32[]{:S(2)}, u32[]{:S(2)}) collective-permute-start(f32[2,8192]{1,0:T(2,128)S(1)} %broadcast.91), channel_id=1, source_target_pairs={{4,0},{8,4},{12,8},{16,12},{20,16},{24,20},{28,24},{32,28},{36,32}... | collective-permute-start | bytes 196616 | tf_op jit(solution)/shard_map/ppermute | solution.py:28
  5.0 23.5 %collective-permute-start.1 = (f32[1,8192]{1,0:T(1,128)}, f32[1,8192]{1,0:T(1,128)}, u32[]{:S(2)}, u32[]{:S(2)}) collective-permute-start(f32[1,8192]{1,0:T(1,128)} %get-tuple-element.102), channel_id=1, source_target_pairs={{0,4},{4,8},{8,12},{12,16},{16,20},{20,24},{24,28},{28,32},{32,36}... | collective-permute-start | bytes 98312 | tf_op jit(solution)/shard_map/ppermute | solution.py:45
  11.2 5.2 %collective-permute-start = (f32[32,1]{1,0:T(8,128)S(1)}, f32[32,1]{1,0:T(8,128)S(1)}, u32[]{:S(2)}, u32[]{:S(2)}) collective-permute-start(f32[32,1]{1,0:T(8,128)S(1)} %get-tuple-element.101), channel_id=1, source_target_pairs={{0,1},{1,2},{2,3},{4,5},{5,6},{6,7},{8,9},{9,10},{10,11},{12,13},{... | collective-permute-start | bytes 392 | tf_op jit(solution)/shard_map/ppermute | solution.py:45
  15.1 5.7 %collective-permute-start.3 = (f32[32,1]{1,0:T(8,128)S(1)}, f32[32,1]{1,0:T(8,128)S(1)}, u32[]{:S(2)}, u32[]{:S(2)}) collective-permute-start(f32[32,1]{1,0:T(8,128)S(1)} %get-tuple-element.100), channel_id=1, source_target_pairs={{1,0},{2,1},{3,2},{5,4},{6,5},{7,6},{9,8},{10,9},{11,10},{13,12},{... | collective-permute-start | bytes 392 | tf_op jit(solution)/shard_map/ppermute | solution.py:46
  16.4 243.2 %copy-start.39 = (pred[34]{0:T(512)(128)(4,1)}, pred[34]{0:T(512)(128)(4,1)S(1)}, u32[]{:S(2)}) copy-start(pred[34]{0:T(512)(128)(4,1)S(1)} %compare_and_fusion) | copy-start | bytes 106
  16.5 12.0 %collective-permute-start.2 = (f32[1,8192]{1,0:T(1,128)}, f32[1,8192]{1,0:T(1,128)S(1)}, u32[]{:S(2)}, u32[]{:S(2)}) collective-permute-start(f32[1,8192]{1,0:T(1,128)} %get-tuple-element.103), channel_id=1, source_target_pairs={{4,0},{8,4},{12,8},{16,12},{20,16},{24,20},{28,24},{32,28},{36,32}... | collective-permute-start | bytes 98312 | tf_op jit(solution)/shard_map/ppermute | solution.py:46
  21.5 7.0 %copy-start.1 = (f32[32,8192]{1,0:T(8,128)S(1)}, f32[32,8192]{1,0:T(8,128)}, u32[]{:S(2)}) copy-start(f32[32,8192]{1,0:T(8,128)} %param.7) | copy-start | bytes 3145732
  22.6 5.9 %copy-start.21 = (f32[36,8192]{1,0:T(8,128)}, f32[36,8192]{1,0:T(8,128)S(1)}, u32[]{:S(2)}) copy-start(f32[36,8192]{1,0:T(8,128)S(1)} %pad_maximum_fusion.49) | copy-start | bytes 3538948
  23.4 9.0 %collective-permute-start.6 = (f32[36,2]{1,0:T(8,128)}, f32[36,2]{1,0:T(8,128)S(1)}, u32[]{:S(2)}, u32[]{:S(2)}) collective-permute-start(f32[36,2]{1,0:T(8,128)} %get-tuple-element.85), channel_id=1, source_target_pairs={{0,1},{1,2},{2,3},{4,5},{5,6},{6,7},{8,9},{9,10},{10,11},{12,13},{... | collective-permute-start | bytes 872 | tf_op jit(solution)/shard_map/ppermute | solution.py:25
  27.2 5.9 %collective-permute-start.7 = (f32[36,2]{1,0:T(8,128)}, f32[36,2]{1,0:T(8,128)S(1)}, u32[]{:S(2)}, u32[]{:S(2)}) collective-permute-start(f32[36,2]{1,0:T(8,128)} %get-tuple-element.84), channel_id=1, source_target_pairs={{1,0},{2,1},{3,2},{5,4},{6,5},{7,6},{9,8},{10,9},{11,10},{13,12},{... | collective-permute-start | bytes 872 | tf_op jit(solution)/shard_map/ppermute | solution.py:28
  35.6 4.1 copy-start.29
  41.0 2.6 collective-permute-start.8
  42.3 4.7 collective-permute-start.9
  48.3 5.4 %collective-permute-start.10 = (f32[36,2]{1,0:T(8,128)S(1)}, f32[36,2]{1,0:T(8,128)S(1)}, u32[]{:S(2)}, u32[]{:S(2)}) collective-permute-start(f32[36,2]{1,0:T(8,128)S(1)} %get-tuple-element.83), channel_id=1, source_target_pairs={{0,1},{1,2},{2,3},{4,5},{5,6},{6,7},{8,9},{9,10},{10,11},{12,13},{... | collective-permute-start | bytes 872 | tf_op jit(solution)/shard_map/ppermute | solution.py:25
  52.2 5.7 %collective-permute-start.11 = (f32[36,2]{1,0:T(8,128)S(1)}, f32[36,2]{1,0:T(8,128)S(1)}, u32[]{:S(2)}, u32[]{:S(2)}) collective-permute-start(f32[36,2]{1,0:T(8,128)S(1)} %get-tuple-element.82), channel_id=1, source_target_pairs={{1,0},{2,1},{3,2},{5,4},{6,5},{7,6},{9,8},{10,9},{11,10},{13,12},{... | collective-permute-start | bytes 872 | tf_op jit(solution)/shard_map/ppermute | solution.py:28
  60.4 4.1 copy-start.7
  110.6 6.9 %copy-start.2 = (f32[32,8192]{1,0:T(8,128)}, f32[32,8192]{1,0:T(8,128)S(1)}, u32[]{:S(2)}) copy-start(f32[32,8192]{1,0:T(8,128)S(1)} %multiply_subtract_fusion.3) | copy-start | bytes 3145732
  110.7 2.6 collective-permute-start.12
  112.0 5.4 %collective-permute-start.13 = (f32[2,8192]{1,0:T(2,128)S(1)}, f32[2,8192]{1,0:T(2,128)S(1)}, u32[]{:S(2)}, u32[]{:S(2)}) collective-permute-start(f32[2,8192]{1,0:T(2,128)S(1)} %get-tuple-element.97), channel_id=1, source_target_pairs={{4,0},{8,4},{12,8},{16,12},{20,16},{24,20},{28,24},{32,28},{36,32}... | collective-permute-start | bytes 196616 | tf_op jit(solution)/shard_map/ppermute | solution.py:28
  118.6 4.4 collective-permute-start.14
  121.5 5.7 %collective-permute-start.15 = (f32[36,2]{1,0:T(8,128)S(1)}, f32[36,2]{1,0:T(8,128)S(1)}, u32[]{:S(2)}, u32[]{:S(2)}) collective-permute-start(f32[36,2]{1,0:T(8,128)S(1)} %get-tuple-element.80), channel_id=1, source_target_pairs={{1,0},{2,1},{3,2},{5,4},{6,5},{7,6},{9,8},{10,9},{11,10},{13,12},{... | collective-permute-start | bytes 872 | tf_op jit(solution)/shard_map/ppermute | solution.py:28
  129.7 4.8 copy-start.3
  129.7 4.8 copy-start.8
  174.7 6.8 %copy-start.13 = (f32[32,8192]{1,0:T(8,128)}, f32[32,8192]{1,0:T(8,128)S(1)}, u32[]{:S(2)}) copy-start(f32[32,8192]{1,0:T(8,128)S(1)} %multiply_subtract_fusion.2) | copy-start | bytes 3145732
  174.8 2.6 collective-permute-start.16
  176.1 5.2 %collective-permute-start.17 = (f32[2,8192]{1,0:T(2,128)S(1)}, f32[2,8192]{1,0:T(2,128)S(1)}, u32[]{:S(2)}, u32[]{:S(2)}) collective-permute-start(f32[2,8192]{1,0:T(2,128)S(1)} %get-tuple-element.95), channel_id=1, source_target_pairs={{4,0},{8,4},{12,8},{16,12},{20,16},{24,20},{28,24},{32,28},{36,32}... | collective-permute-start | bytes 196616 | tf_op jit(solution)/shard_map/ppermute | solution.py:28
  182.6 5.4 %collective-permute-start.18 = (f32[36,2]{1,0:T(8,128)S(1)}, f32[36,2]{1,0:T(8,128)S(1)}, u32[]{:S(2)}, u32[]{:S(2)}) collective-permute-start(f32[36,2]{1,0:T(8,128)S(1)} %get-tuple-element.79), channel_id=1, source_target_pairs={{0,1},{1,2},{2,3},{4,5},{5,6},{6,7},{8,9},{9,10},{10,11},{12,13},{... | collective-permute-start | bytes 872 | tf_op jit(solution)/shard_map/ppermute | solution.py:25
  186.5 5.7 %collective-permute-start.19 = (f32[36,2]{1,0:T(8,128)S(1)}, f32[36,2]{1,0:T(8,128)S(1)}, u32[]{:S(2)}, u32[]{:S(2)}) collective-permute-start(f32[36,2]{1,0:T(8,128)S(1)} %get-tuple-element.78), channel_id=1, source_target_pairs={{1,0},{2,1},{3,2},{5,4},{6,5},{7,6},{9,8},{10,9},{11,10},{13,12},{... | collective-permute-start | bytes 872 | tf_op jit(solution)/shard_map/ppermute | solution.py:28
  194.7 4.8 copy-start.9
  194.7 4.8 copy-start.14
  240.3 6.9 %copy-start.15 = (f32[32,8192]{1,0:T(8,128)}, f32[32,8192]{1,0:T(8,128)S(1)}, u32[]{:S(2)}) copy-start(f32[32,8192]{1,0:T(8,128)S(1)} %multiply_add_fusion) | copy-start | bytes 3145732
  240.4 2.6 collective-permute-start.20
  241.7 5.4 %collective-permute-start.21 = (f32[2,8192]{1,0:T(2,128)S(1)}, f32[2,8192]{1,0:T(2,128)S(1)}, u32[]{:S(2)}, u32[]{:S(2)}) collective-permute-start(f32[2,8192]{1,0:T(2,128)S(1)} %get-tuple-element.93), channel_id=1, source_target_pairs={{4,0},{8,4},{12,8},{16,12},{20,16},{24,20},{28,24},{32,28},{36,32}... | collective-permute-start | bytes 196616 | tf_op jit(solution)/shard_map/ppermute | solution.py:28
  247.1 4.2 copy-start.36
  247.3 5.6 %collective-permute-start.22 = (f32[36,2]{1,0:T(8,128)S(1)}, f32[36,2]{1,0:T(8,128)S(1)}, u32[]{:S(2)}, u32[]{:S(2)}) collective-permute-start(f32[36,2]{1,0:T(8,128)S(1)} %get-tuple-element.77), channel_id=1, source_target_pairs={{0,1},{1,2},{2,3},{4,5},{5,6},{6,7},{8,9},{9,10},{10,11},{12,13},{... | collective-permute-start | bytes 872 | tf_op jit(solution)/shard_map/ppermute | solution.py:25
  251.2 8.4 %copy-start.16 = (f32[32,8192]{1,0:T(8,128)S(1)}, f32[32,8192]{1,0:T(8,128)}, u32[]{:S(2)}) copy-start(f32[32,8192]{1,0:T(8,128)} %copy-done.15) | copy-start | bytes 3145732
  251.2 5.8 %collective-permute-start.23 = (f32[36,2]{1,0:T(8,128)S(1)}, f32[36,2]{1,0:T(8,128)S(1)}, u32[]{:S(2)}, u32[]{:S(2)}) collective-permute-start(f32[36,2]{1,0:T(8,128)S(1)} %get-tuple-element.76), channel_id=1, source_target_pairs={{1,0},{2,1},{3,2},{5,4},{6,5},{7,6},{9,8},{10,9},{11,10},{13,12},{... | collective-permute-start | bytes 872 | tf_op jit(solution)/shard_map/ppermute | solution.py:28
  259.6 4.2 copy-start.10
  259.6 4.2 copy-start.17
  259.6 4.2 copy-start.30
  263.8 7.6 %copy-start.38 = (s32[1024]{0:T(1024)S(1)}, s32[1024]{0:T(1024)}, u32[]{:S(2)}) copy-start(s32[1024]{0:T(1024)} %param.9) | copy-start | bytes 12292
  265.9 25.0 %copy-start.4 = (f32[32,8192]{1,0:T(8,128)}, f32[32,8192]{1,0:T(8,128)S(1)}, u32[]{:S(2)}) copy-start(f32[32,8192]{1,0:T(8,128)S(1)} %get-tuple-element.66) | copy-start | bytes 3145732
  266.7 5.4 %collective-permute-start.24 = (f32[2,8192]{1,0:T(2,128)}, f32[2,8192]{1,0:T(2,128)S(1)}, u32[]{:S(2)}, u32[]{:S(2)}) collective-permute-start(f32[2,8192]{1,0:T(2,128)} %get-tuple-element.90), channel_id=1, source_target_pairs={{0,4},{4,8},{8,12},{12,16},{16,20},{20,24},{24,28},{28,32},{32,36}... | collective-permute-start | bytes 196616 | tf_op jit(solution)/shard_map/ppermute | solution.py:25
  270.1 4.4 collective-permute-start.25
  272.1 7.7 %copy-start.37 = (s32[8,128]{0,1:T(8,128)S(1)}, s32[8,128]{0,1:T(8,128)}, u32[]{:S(2)}) copy-start(s32[8,128]{0,1:T(8,128)} %copy.9) | copy-start | bytes 12292
  276.6 4.2 collective-permute-start.26
  278.6 5.7 %collective-permute-start.27 = (f32[36,2]{1,0:T(8,128)S(1)}, f32[36,2]{1,0:T(8,128)S(1)}, u32[]{:S(2)}, u32[]{:S(2)}) collective-permute-start(f32[36,2]{1,0:T(8,128)S(1)} %get-tuple-element.74), channel_id=1, source_target_pairs={{1,0},{2,1},{3,2},{5,4},{6,5},{7,6},{9,8},{10,9},{11,10},{13,12},{... | collective-permute-start | bytes 872 | tf_op jit(solution)/shard_map/ppermute | solution.py:28
  286.8 4.1 copy-start.18
  331.8 3.3 collective-permute-start.28
  333.1 5.7 %collective-permute-start.29 = (f32[2,8192]{1,0:T(2,128)}, f32[2,8192]{1,0:T(2,128)}, u32[]{:S(2)}, u32[]{:S(2)}) collective-permute-start(f32[2,8192]{1,0:T(2,128)} %get-tuple-element.89), channel_id=1, source_target_pairs={{4,0},{8,4},{12,8},{16,12},{20,16},{24,20},{28,24},{32,28},{36,32}... | collective-permute-start | bytes 196616 | tf_op jit(solution)/shard_map/ppermute | solution.py:28
  335.1 9.7 %copy-start.31 = (s32[128,8,128]{0,1,2:T(8,128)S(1)}, s32[128,8,128]{0,1,2:T(8,128)}, u32[]{:S(2)}) copy-start(s32[128,8,128]{0,1,2:T(8,128)} %fusion.54) | copy-start | bytes 1572868
  340.9 4.8 collective-permute-start.30
  343.5 5.7 %collective-permute-start.31 = (f32[36,2]{1,0:T(8,128)S(1)}, f32[36,2]{1,0:T(8,128)S(1)}, u32[]{:S(2)}, u32[]{:S(2)}) collective-permute-start(f32[36,2]{1,0:T(8,128)S(1)} %get-tuple-element.72), channel_id=1, source_target_pairs={{1,0},{2,1},{3,2},{5,4},{6,5},{7,6},{9,8},{10,9},{11,10},{13,12},{... | collective-permute-start | bytes 872 | tf_op jit(solution)/shard_map/ppermute | solution.py:28
  351.7 4.1 copy-start.19
  395.1 6.2 %copy-start.32 = (s32[128,8,128]{0,2,1:T(8,128)S(1)}, s32[128,8,128]{0,2,1:T(8,128)}, u32[]{:S(2)}) copy-start(s32[128,8,128]{0,2,1:T(8,128)} %copy.10) | copy-start | bytes 1572868
  398.7 3.6 collective-permute-start.32
  400.0 5.7 %collective-permute-start.33 = (f32[2,8192]{1,0:T(2,128)}, f32[2,8192]{1,0:T(2,128)}, u32[]{:S(2)}, u32[]{:S(2)}) collective-permute-start(f32[2,8192]{1,0:T(2,128)} %get-tuple-element.87), channel_id=1, source_target_pairs={{4,0},{8,4},{12,8},{16,12},{20,16},{24,20},{28,24},{32,28},{36,32}... | collective-permute-start | bytes 196616 | tf_op jit(solution)/shard_map/ppermute | solution.py:28
  408.9 5.5 %collective-permute-start.34 = (f32[36,2]{1,0:T(8,128)}, f32[36,2]{1,0:T(8,128)S(1)}, u32[]{:S(2)}, u32[]{:S(2)}) collective-permute-start(f32[36,2]{1,0:T(8,128)} %get-tuple-element.71), channel_id=1, source_target_pairs={{0,1},{1,2},{2,3},{4,5},{5,6},{6,7},{8,9},{9,10},{10,11},{12,13},{... | collective-permute-start | bytes 872 | tf_op jit(solution)/shard_map/ppermute | solution.py:25
  412.6 5.9 %collective-permute-start.35 = (f32[36,2]{1,0:T(8,128)}, f32[36,2]{1,0:T(8,128)S(1)}, u32[]{:S(2)}, u32[]{:S(2)}) collective-permute-start(f32[36,2]{1,0:T(8,128)} %get-tuple-element.70), channel_id=1, source_target_pairs={{1,0},{2,1},{3,2},{5,4},{6,5},{7,6},{9,8},{10,9},{11,10},{13,12},{... | collective-permute-start | bytes 872 | tf_op jit(solution)/shard_map/ppermute | solution.py:28
  421.0 4.7 copy-start.12
  421.0 4.7 copy-start.20
  425.7 38.0 %copy-start.5 = (f32[32,8192]{1,0:T(8,128)S(1)}, f32[32,8192]{1,0:T(8,128)}, u32[]{:S(2)}) copy-start(f32[32,8192]{1,0:T(8,128)} %copy-done.4) | copy-start | bytes 3145732
  (12 other events, 19.5 us)
where the time goes:
time: 516 us; the launch traced here: 507 us
  blocking collectives  234 us (45%)
  other arithmetic  83.9 us (16%)
  starting transfers between devices  71.9 us (14%)
  waiting for transfers between devices  56.1 us (11%)
  local copies, waits for them, and re-layouts  40.5 us (8%)
  between operations  20.5 us (4%)
    psum x28, blocking collectives, one_axis_at_a_time(): return functools.reduce(lax.psum, axes, array)  234 us
    ppermute x16, waiting for transfers between devices, padded_2(): lax.ppermute(lax.slice_in_dim(block, 0, width, axis=dim), axis, backward)  53.3 us
    ppermute x16, starting transfers between devices, padded_2(): lax.ppermute(lax.slice_in_dim(block, block.shape[dim] - width, None, axis...  38.9 us
    mul x8, other arithmetic, wide_apply(): ((kappa_wide + 4.0) * padded[1:-1, 1:-1] - neighbours(padded)) * inside  34.8 us
    ppermute x16, starting transfers between devices, padded_2(): lax.ppermute(lax.slice_in_dim(block, 0, width, axis=dim), axis, backward)  21.2 us
    concatenate x8, local copies, waits for them, and re-layouts, padded_2(): block = jnp.concatenate([low, block, high], axis=dim)  20.2 us
    reduce_sum x6, other arithmetic, paired(): jnp.sum(residual * image)  14.9 us
  transfers between devices with their start and end apart: 36, of which 19 were waited for; matrix products, arithmetic and copies ran while one was open for 3% of the time, Pallas kernels for 0%

commit v1 on v0

v1 whole, which is shorter than its diff:
```python
import jax
import jax.numpy as jnp
from jax import lax
from jax.experimental import pallas as pl
from jax.experimental.pallas import tpu as pltpu
from jax.sharding import PartitionSpec as P

TILE = 128
OWNED_MOST = 15
MESH = pl.DeviceIdType.MESH
F32 = jnp.float32

ROWS, TILES, TOP, BOTTOM, SLOTS, DEEP = 32, 8, 8, 40, 48, 5
PITCH = TILES * 8
THETA = (0.0, 2.0)
SIGMA = (1.0, 2.0**-24)
TINY = 3e-7


def kernel(
    dims, counts_h, offset_h, kappa_h, labels_h, owner_h, mode_h, owned_ref,
    st_c, st_o, st_k, off_m, cnt_m, kap_m, kap_g, w_m, w_g, r_m, r_g, t_m, t_g,
    a_m, a_g, b_m, b_g, q_m, mode_m, pack, e_off, e_cnt, e_kap, e_a, e_b, e_q, e_r, e_w, e_k,
    lab, own, pick, src1, src2, got1, got2,
    ld_sem, small_sem, row_s, row_r, edge_s, edge_r, lab_s, lab_r, s1, r1, s2, r2, out_sem,
):
    strips, subs = dims
    strip, sub = lax.axis_index("strip"), lax.axis_index("sub")
    core, chip = lax.rem(strip, 2), lax.div(strip, 2)
    chips, near = strips // 2, 2 * subs
    me1 = core * subs + sub
    up, down = lax.rem(strip + strips - 1, strips), lax.rem(strip + 1, strips)
    left, right = lax.rem(sub + subs - 1, subs), lax.rem(sub + 1, subs)
    first, last = strip == 0, strip == strips - 1

    def peer1(k):
        j = lax.rem(me1 + k, near)
        return j, (strip - core + lax.div(j, subs), lax.rem(j, subs))

    def peer2(k):
        j = lax.rem(chip + k, chips)
        return j, (j * 2 + core, sub)

    def each(low, high, do):
        def step(k, carry):
            do(k)
            return carry

        lax.fori_loop(low, high, step, 0)

    barrier = pltpu.get_barrier_semaphore()

    def greet(device):
        pl.semaphore_signal(barrier, inc=1, device_id=device, device_id_type=MESH)

    each(1, near, lambda k: greet(peer1(k)[1]))
    each(1, chips, lambda k: greet(peer2(k)[1]))
    around = [
        (up, sub), (down, sub), (strip, left), (strip, right),
        (up, left), (down, left), (up, right), (down, right),
    ]
    for device in around:
        greet(device)

    order = (0, 3, 1, 2)
    loads = {}
    for i in order:
        for n, (hbm, stage) in enumerate(((offset_h, st_o), (counts_h, st_c), (kappa_h, st_k))):
            loads[i, n] = pltpu.make_async_copy(
                hbm.at[pl.ds(8 * i, 8), :], stage.at[pl.ds(8 * i, 8), :], ld_sem.at[3 * i + n]
            )
            loads[i, n].start()
    load_owner = pltpu.make_async_copy(owner_h, own, small_sem.at[0])
    load_owner.start()
    load_labels = pltpu.make_async_copy(labels_h, lab.at[sub], small_sem.at[1])
    load_labels.start()

    lane = lax.broadcasted_iota(jnp.int32, (8, 128), 1)
    sublane = lax.broadcasted_iota(jnp.int32, (8, 128), 0)

    def at(q, t):
        return pl.ds(pl.multiple_of(q * PITCH + t * 8, 8), 8)

    def ghost_at(q):
        return pl.ds(pl.multiple_of(q * 8, 8), 8)

    def relayout(i):
        for n in range(3):
            loads[i, n].wait()

        def one(s):
            for t in range(TILES):
                from_ = (pl.ds(8 * i, 8), pl.ds(pl.multiple_of(s * 1024 + t * 128, 128), 128))
                to = (pl.ds((TOP + 8 * i) * PITCH + t * 8 + s, 8, stride=PITCH), slice(None))
                off, cnt, kap = st_o[from_], st_c[from_].astype(F32), st_k[from_]
                weight = jnp.exp(off)
                off_m[to] = off
                cnt_m[to] = cnt
                kap_m[to] = kap + 4.0
                w_m[to] = weight
                r_m[to] = cnt - weight

        each(0, 8, one)

    def remote(src, dst, send, recv, device):
        return pltpu.make_async_remote_copy(
            src_ref=src, dst_ref=dst, send_sem=send, recv_sem=recv,
            device_id=device, device_id_type=MESH,
        )

    def row_copies(field, n, low, high):
        many = (high - low) * PITCH
        return [
            remote(
                field.at[pl.ds((TOP + low) * PITCH, many), :],
                field.at[pl.ds((BOTTOM + low) * PITCH, many), :],
                row_s.at[2 * n], row_r.at[2 * n], (up, sub),
            ),
            remote(
                field.at[pl.ds((BOTTOM - high) * PITCH, many), :],
                field.at[pl.ds((TOP - high) * PITCH, many), :],
                row_s.at[2 * n + 1], row_r.at[2 * n + 1], (down, sub),
            ),
        ]

    def edge_copies(leftmost, rightmost, edges, n):
        made = []
        for side, source, beside in ((1, leftmost, left), (0, rightmost, right)):
            to = edges.at[side]
            for m, (rows, landing, device) in enumerate((
                (pl.ds(0, 32), pl.ds(8, 32), (strip, beside)),
                (pl.ds(0, 8), pl.ds(40, 8), (up, beside)),
                (pl.ds(24, 8), pl.ds(0, 8), (down, beside)),
            )):
                k = 6 * n + 3 * side + m
                made.append(
                    remote(source(rows), to.at[landing, :], edge_s.at[k], edge_r.at[k], device)
                )
        return made

    def hbm_edges(hbm, edges, n):
        wide = TILES * 1024
        return edge_copies(
            lambda rows: hbm.at[rows, pl.ds(0, 128)],
            lambda rows: hbm.at[rows, pl.ds(wide - 128, 128)],
            edges, n,
        )

    def packed_edges(field, edges, n):
        for g in range(4):
            base = (TOP + 8 * g) * PITCH
            pack[n - 3, 0, pl.ds(8 * g, 8), :] = field[pl.ds(base, 8, stride=PITCH), :]
            pack[n - 3, 1, pl.ds(8 * g, 8), :] = field[pl.ds(base + PITCH - 1, 8, stride=PITCH), :]
        return edge_copies(
            lambda rows: pack.at[n - 3, 0, rows, :], lambda rows: pack.at[n - 3, 1, rows, :],
            edges, n,
        )

    def start(copies):
        for copy in copies:
            copy.start()

    def arrived(copies):
        for copy in copies:
            copy.wait_recv()

    def sent(copies):
        for copy in copies:
            copy.wait_send()

    left_open = jnp.where(sub > 0, 1.0, 0.0).astype(F32)
    right_open = jnp.where(sub < subs - 1, 1.0, 0.0).astype(F32)
    open_ = jnp.where(
        (sublane == 0) & (lane >= 64), left_open,
        jnp.where((sublane == 7) & (lane < 64), right_open, 1.0),
    )

    def row(main, ghost, q):
        return [main[at(q, t), :] for t in range(TILES)] + [ghost[ghost_at(q), :]]

    def put(main, ghost, q, values):
        for t in range(TILES):
            main[at(q, t), :] = values[t]
        ghost[ghost_at(q), :] = values[TILES]

    def stencil(above, here, below, kap):
        before = [pltpu.roll(v, 1, axis=1) for v in here]
        after = [pltpu.roll(v, 127, axis=1) for v in here]
        done = []
        for t in range(TILES + 1):
            beside = jnp.where(lane == 0, before[t - 1], before[t]) + jnp.where(
                lane == 127, after[(t + 1) % (TILES + 1)], after[t]
            )
            done.append(kap[t] * here[t] - ((above[t] + below[t]) + beside))
        done[TILES] = done[TILES] * open_
        return done

    def rows_of_k(main, ghost, q, many):
        window = [row(main, ghost, q - 1 + n) for n in range(many + 2)]
        return [
            stencil(window[n], window[n + 1], window[n + 2], row(kap_m, kap_g, q + n))
            for n in range(many)
        ], window[1:-1]

    def blank(main, ghost, low, high):
        zero = jnp.zeros((8, 128), F32)

        @pl.when(first)
        def _():
            for q in range(low, TOP):
                put(main, ghost, q, [zero] * 9)

        @pl.when(last)
        def _():
            for q in range(BOTTOM, high):
                put(main, ghost, q, [zero] * 9)

    def apply_k(main, ghost, out, out_g, low, high):
        def two(n):
            q = low + 2 * n
            made, _ = rows_of_k(main, ghost, q, 2)
            for m in range(2):
                put(out, out_g, q + m, made[m])

        each(0, (high - low) // 2, two)
        blank(out, out_g, low, high)

    def added(products):
        while len(products) > 1:
            products = [a + b for a, b in zip(products[::2], products[1::2])]
        return products[0]

    def shifted(base, base_g, out, out_g, low, high, theta, sigma, sums):
        def make(q, many):
            made, _ = rows_of_k(t_m, t_g, q, many)
            results = []
            for m in range(many):
                weight, values = row(w_m, w_g, q + m), row(base, base_g, q + m)
                got = [
                    (0.1 * sigma) * made[m][t] + (sigma * (weight[t] - theta)) * values[t]
                    for t in range(9)
                ]
                put(out, out_g, q + m, got)
                results.append((got, values))
            return results

        each(low, TOP, lambda q: make(q, 1) and None)
        each(BOTTOM, high, lambda q: make(q, 1) and None)

        def two(n, carry):
            q = TOP + 2 * n
            for m, (got, values) in enumerate(make(q, 2)):
                carry = sums(carry, got, values, q + m)
            return carry

        zero = jnp.zeros((8, 128), F32)
        total = lax.fori_loop(0, ROWS // 2, two, (zero,) * 3)
        blank(out, out_g, low, high)
        return total

    def inject(main, ghost, edges, masked=False):
        def one(q):
            ghost[ghost_at(q), :] = jnp.where(
                lane < 64,
                pltpu.roll(main[at(q, 0), :], 7, axis=0),
                pltpu.roll(main[at(q, TILES - 1), :], 1, axis=0),
            )

        each(TOP - DEEP, BOTTOM + DEEP, one)
        for g in range(SLOTS // 8):
            for side, s in ((0, 0), (1, 7)):
                where = (pl.ds(g * 64 + s, 8, stride=8), slice(None))
                mine = lane >= 64 if side == 0 else lane < 64
                fresh = edges[side, pl.ds(8 * g, 8), :]
                if masked:
                    fresh = fresh * (left_open if side == 0 else right_open)
                ghost[where] = jnp.where(mine, fresh, ghost[where])

    def hop1(u):
        def go(k):
            _, device = peer1(k)
            remote(
                src1.at[u], got1.at[near * u + me1],
                s1.at[near * u + k], r1.at[near * u + me1], device,
            ).start()

        each(1, near, go)

    def hop1_done(u):
        def wait(k):
            j, device = peer1(k)
            remote(
                src1.at[u], got1.at[near * u + j],
                s1.at[near * u + k], r1.at[near * u + j], device,
            ).wait()

        each(1, near, wait)

    def hop2(u):
        def go(k):
            _, device = peer2(k)
            remote(
                src2.at[u], got2.at[chips * u + chip],
                s2.at[chips * u + k], r2.at[chips * u + chip], device,
            ).start()

        each(1, chips, go)

    def hop2_done(u):
        def wait(k):
            j, device = peer2(k)
            remote(
                src2.at[u], got2.at[chips * u + j],
                s2.at[chips * u + k], r2.at[chips * u + j], device,
            ).wait()

        each(1, chips, wait)

    def over_sublanes(v):
        for n in (4, 2, 1):
            v = v + pltpu.roll(v, n, axis=0)
        return v

    def moments_out(u, sums):
        message = jnp.zeros((8, 128), F32)
        for n, v in enumerate(sums):
            message = jnp.where(sublane == n, over_sublanes(v), message)
        src1[u] = message
        got1[near * u + me1] = message
        hop1(u)

    def moments_on(u):
        hop1_done(u)
        total = got1[near * u]
        for j in range(1, near):
            total = total + got1[near * u + j]
        both = jnp.concatenate([total, jnp.zeros((8, 128), F32)], axis=0)
        src2[u] = both
        got2[chips * u + chip] = both
        hop2(u)

    def moments_in(u):
        hop2_done(u)
        total = got2[chips * u, 0:8, :]
        for j in range(1, chips):
            total = total + got2[chips * u + j, 0:8, :]
        flat = jnp.sum(total, axis=1, keepdims=True)
        return [jnp.broadcast_to(flat[n : n + 1, :], (8, 128)) for n in range(7)]

    def solve(moments, sigma):
        g00, g01, g11, g02, g12, g22, h22 = moments
        inverse = 1.0 / sigma
        a00 = inverse * g01 + THETA[0] * g00
        a01 = inverse * g02 + THETA[1] * g01
        a11 = inverse * g12 + THETA[1] * g11
        a02 = inverse * g12 + THETA[0] * g02
        a12 = inverse * g22 + THETA[1] * g12
        a22 = h22
        i0 = 1.0 / a00
        l10, l20 = a01 * i0, a02 * i0
        d1, u12 = a11 - l10 * a01, a12 - l10 * a02
        i1 = jnp.where(d1 > TINY * a11, 1.0 / d1, 0.0)
        l21 = u12 * i1
        d2 = a22 - l20 * a02 - l21 * u12
        i2 = jnp.where(d2 > TINY * a22, 1.0 / d2, 0.0)
        y0 = g00
        y1 = g01 - l10 * y0
        y2 = g02 - l20 * y0 - l21 * y1
        c2 = y2 * i2
        c1 = y1 * i1 - l21 * c2
        c0 = y0 * i0 - l10 * c1 - l20 * c2
        return c0, c1, c2

    relayout(order[0])
    relayout(order[1])
    pl.semaphore_wait(barrier, near - 1 + chips - 1 + len(around))
    halo = row_copies(off_m, 0, 0, 5) + row_copies(cnt_m, 1, 0, 5) + row_copies(kap_m, 2, 0, 4)
    rims = hbm_edges(offset_h, e_off, 0) + hbm_edges(counts_h, e_cnt, 1) + hbm_edges(kappa_h, e_kap, 2)
    start(halo)
    start(rims)
    load_labels.wait()

    def label_copy(k, arriving):
        z = lax.rem(sub + k, subs)
        held = z if arriving else sub
        return remote(labels_h, lab.at[held], lab_s.at[k], lab_r.at[held], (strip, z))

    for k in range(1, subs):
        label_copy(k, False).start()
    relayout(order[2])
    relayout(order[3])
    arrived(halo)
    arrived(rims)

    def halo_rows(do):
        each(TOP - DEEP, TOP, do)
        each(BOTTOM, BOTTOM + DEEP, do)

    def prime(q):
        for t in range(TILES):
            weight = jnp.exp(off_m[at(q, t), :])
            w_m[at(q, t), :] = weight
            r_m[at(q, t), :] = cnt_m[at(q, t), :] - weight

    halo_rows(prime)
    for side, alive in ((0, left_open), (1, right_open)):
        weight = jnp.exp(e_off[side])
        e_w[side] = weight
        e_r[side] = (e_cnt[side].astype(F32) - weight) * alive
        e_k[side] = e_kap[side] + 4.0
    inject(kap_m, kap_g, e_k)
    inject(w_m, w_g, e_w)
    inject(r_m, r_g, e_r)
    blank(r_m, r_g, TOP - DEEP, BOTTOM + DEEP)

    def basis(n):
        sigma = SIGMA[n]
        apply_k(r_m, r_g, t_m, t_g, 4, 44)

        def sums_a(carry, got, values, q):
            return (
                carry[0] + added([v * v for v in values[:8]]),
                carry[1] + added([v * g for v, g in zip(values[:8], got[:8])]),
                carry[2] + added([g * g for g in got[:8]]),
            )

        g00, g01, g11 = shifted(r_m, r_g, a_m, a_g, 5, 43, THETA[0], sigma, sums_a)
        moving = []
        if n == 0:
            moving = row_copies(a_m, 3, 3, 5) + packed_edges(a_m, e_a, 3)
            start(moving)
        apply_k(a_m, a_g, t_m, t_g, 6, 42)

        def sums_b(carry, got, values, q):
            start_ = row(r_m, r_g, q)
            return (
                carry[0] + added([v * g for v, g in zip(start_[:8], got[:8])]),
                carry[1] + added([v * g for v, g in zip(values[:8], got[:8])]),
                carry[2] + added([g * g for g in got[:8]]),
            )

        g02, g12, g22 = shifted(a_m, a_g, b_m, b_g, 7, 41, THETA[1], sigma, sums_b)
        if n == 0:
            more = row_copies(b_m, 4, 1, 5) + packed_edges(b_m, e_b, 4)
            start(more)
            moving = moving + more

        def energy(m, carry):
            q = TOP + 2 * m
            made, values = rows_of_k(b_m, b_g, q, 2)
            for k in range(2):
                weight = [w_m[at(q + k, t), :] for t in range(TILES)]
                carry = carry + added([
                    0.1 * (made[k][t] * made[k][t]) + weight[t] * (values[k][t] * values[k][t])
                    for t in range(TILES)
                ])
            return carry

        h22 = lax.fori_loop(0, ROWS // 2, energy, jnp.zeros((8, 128), F32))
        moments_out(n, (g00, g01, g11, g02, g12, g22, h22))
        return moving

    moving = basis(0)
    moments_on(0)

    arrived(moving)
    inject(b_m, b_g, e_b, masked=True)
    blank(b_m, b_g, TOP - DEEP, BOTTOM + DEEP)
    apply_k(b_m, b_g, t_m, t_g, 7, 41)

    def second_k(n):
        q = TOP + 2 * n
        made, _ = rows_of_k(t_m, t_g, q, 2)
        for m in range(2):
            for t in range(TILES):
                q_m[at(q + m, t), :] = 0.1 * made[m][t]

    each(0, ROWS // 2, second_k)
    final = row_copies(q_m, 5, 0, 5) + packed_edges(q_m, e_q, 5)
    start(final)
    sent(moving)

    c0, c1, c2 = solve(moments_in(0), SIGMA[0])

    def renew(off, cnt, weight, r, a, b, qb):
        step = c0 * r + (c1 * a + c2 * b)
        q_mode = c0 * (a + (THETA[0] - weight) * r) + (
            c1 * (b + (THETA[1] - weight) * a) + c2 * qb
        )
        fresh = jnp.exp(off + step)
        return step, fresh, cnt - fresh - q_mode

    def renew_row(q, keep):
        for t in range(TILES):
            k = (at(q, t), slice(None))
            step, fresh, gradient = renew(
                off_m[k], cnt_m[k], w_m[k], r_m[k], a_m[k], b_m[k], q_m[k]
            )
            if keep:
                mode_m[k] = step
            w_m[k] = fresh
            r_m[k] = gradient

    each(TOP, BOTTOM, lambda q: renew_row(q, True))
    arrived(final)
    halo_rows(lambda q: renew_row(q, False))
    for side, alive in ((0, left_open), (1, right_open)):
        for g in range(SLOTS // 8):
            k = (side, pl.ds(8 * g, 8), slice(None))
            _, fresh, gradient = renew(
                e_off[k], e_cnt[k].astype(F32), e_w[k], e_r[k], e_a[k], e_b[k], e_q[k]
            )
            e_w[k] = fresh
            e_r[k] = gradient * alive
    inject(w_m, w_g, e_w)
    inject(r_m, r_g, e_r)
    blank(r_m, r_g, TOP - DEEP, BOTTOM + DEEP)

    basis(1)
    moments_on(1)

    sent(final)
    sent(halo)
    sent(rims)
    for k in range(1, subs):
        label_copy(k, True).wait()
    load_owner.wait()
    myself = strip * subs + sub
    mark = jnp.where(own[...] == myself, 1, 0)
    count = mark
    for n in (1, 2, 4, 8, 16, 32, 64):
        count = count + jnp.where(lane >= n, pltpu.roll(count, n, axis=1), 0)
    whole = jnp.broadcast_to(count[:, 127:128], (8, 128))
    below = jnp.where(sublane >= 1, pltpu.roll(whole, 1, axis=0), 0)
    for n in (1, 2, 4):
        below = below + jnp.where(sublane >= n, pltpu.roll(below, n, axis=0), 0)
    slot = jnp.where(mark == 1, count + below - 1, -1)
    region = (sublane * 128 + lane).astype(F32)
    tiles = [
        jnp.concatenate([lab[2 * h], lab[2 * h + 1]], axis=1).astype(F32) for h in range(2)
    ]
    for s in range(OWNED_MOST):
        mine = jnp.max(jnp.where(slot == s, region, -1.0), axis=1, keepdims=True)
        mine = jnp.max(mine, axis=0, keepdims=True)
        for h in range(2):
            pick[s, pl.ds(8 * h, 8), :] = jnp.where(tiles[h] == mine, 1.0, 0.0)

    c0, c1, c2 = solve(moments_in(1), SIGMA[1])

    def finish(q, carry):
        sums = []
        for t in range(TILES):
            k = (at(q, t), slice(None))
            mode = mode_m[k] + (c0 * r_m[k] + (c1 * a_m[k] + c2 * b_m[k]))
            mode_m[k] = mode
            sums.append(carry[t] + jnp.exp(off_m[k] + mode))
        return tuple(sums)

    zero = jnp.zeros((8, 128), F32)
    sums = lax.fori_loop(TOP, BOTTOM, finish, (zero,) * TILES)
    square = zero
    for t in range(TILES):
        square = jnp.where(lane == t, jnp.sum(sums[t], axis=1, keepdims=True), square)
    line = over_sublanes(pltpu.roll(square, 0, axis=1, stride=8, stride_axis=0))
    line = jnp.where(lax.rem(sub, 2) == 1, pltpu.roll(line, 64, axis=1), line)
    message = jnp.where(sublane == lax.div(strip, TILE // ROWS), line, 0.0) * (1.0 / (TILE * TILE))
    src1[2] = message
    got1[near * 2 + me1] = message
    hop1(2)

    outs = []

    def write_out(i):
        def one(s):
            for t in range(TILES):
                st_o[pl.ds(8 * i, 8), pl.ds(pl.multiple_of(s * 1024 + t * 128, 128), 128)] = mode_m[
                    pl.ds((TOP + 8 * i) * PITCH + t * 8 + s, 8, stride=PITCH), :
                ]

        each(0, 8, one)
        outs.append(
            pltpu.make_async_copy(
                st_o.at[pl.ds(8 * i, 8), :], mode_h.at[pl.ds(8 * i, 8), :], out_sem.at[i]
            )
        )
        outs[-1].start()

    write_out(0)
    write_out(1)
    hop1_done(2)
    both = []
    for h in range(2):
        slots = [c * subs + z for c in range(2) for z in (2 * h, 2 * h + 1)]
        both.append(added([got1[near * 2 + j] for j in slots]))
    both = jnp.concatenate(both, axis=0)
    src2[2] = both
    got2[chips * 2 + chip] = both
    hop2(2)
    write_out(2)
    write_out(3)
    hop2_done(2)
    total = got2[chips * 2]
    for j in range(1, chips):
        total = total + got2[chips * 2 + j]
    answer = jnp.zeros((8, 128), F32)
    for h in range(2):
        gathered = zero
        for s in range(8 * h, min(8 * h + 8, OWNED_MOST)):
            both = total * pick[s]
            gathered = jnp.where(
                sublane == s - 8 * h, over_sublanes(both[0:8] + both[8:16]), gathered
            )
        flat = jnp.sum(gathered, axis=1, keepdims=True)
        answer = answer + jnp.where(lane == sublane + 8 * h, flat, 0.0)
    owned_ref[...] = over_sublanes(answer)[0:1, 0:OWNED_MOST]
    for copy in outs:
        copy.wait()


def solution(mesh):
    strips, subs = mesh.shape["strip"], mesh.shape["sub"]
    near, chips = 2 * subs, strips // 2

    def body(counts, offset, kappa, labels, owner):
        height, width = offset.shape
        main = pltpu.VMEM((SLOTS * PITCH, 128), F32)
        ghost = pltpu.VMEM((SLOTS * 8, 128), F32)
        edge = pltpu.VMEM((2, SLOTS, 128), F32)
        dma = pltpu.SemaphoreType.DMA
        anywhere = pl.BlockSpec(memory_space=pl.ANY)
        mode, owned = pl.pallas_call(
            lambda *refs: kernel((strips, subs), *refs),
            out_shape=(
                jax.ShapeDtypeStruct((height, width), F32),
                jax.ShapeDtypeStruct((1, OWNED_MOST), F32),
            ),
            in_specs=[anywhere] * 5,
            out_specs=(anywhere, pl.BlockSpec(memory_space=pltpu.VMEM)),
            scratch_shapes=[
                pltpu.VMEM((height, width), jnp.int32),
                pltpu.VMEM((height, width), F32),
                pltpu.VMEM((height, width), F32),
                main, main, main, ghost, main, ghost, main, ghost, main, ghost,
                main, ghost, main, ghost, main, main,
                pltpu.VMEM((3, 2, 32, 128), F32),
                edge, pltpu.VMEM((2, SLOTS, 128), jnp.int32), edge,
                edge, edge, edge, edge, edge, edge,
                pltpu.VMEM((subs, 8, labels.shape[1]), jnp.int32),
                pltpu.VMEM((8, 128), jnp.int32),
                pltpu.VMEM((OWNED_MOST, 16, 128), F32),
                pltpu.VMEM((3, 8, 128), F32),
                pltpu.VMEM((3, 16, 128), F32),
                pltpu.VMEM((3 * near, 8, 128), F32),
                pltpu.VMEM((3 * chips, 16, 128), F32),
                dma((12,)), dma((2,)), dma((12,)), dma((12,)), dma((36,)), dma((36,)),
                dma((subs,)), dma((subs,)), dma((3 * near,)), dma((3 * near,)),
                dma((3 * chips,)), dma((3 * chips,)), dma((4,)),
            ],
            compiler_params=pltpu.CompilerParams(
                collective_id=0, has_side_effects=True, vmem_limit_bytes=63 << 20
            ),
        )(counts, offset, kappa, labels, owner.reshape(8, 128))
        return mode, owned.reshape(OWNED_MOST)

    return jax.shard_map(
        body,
        mesh=mesh,
        in_specs=(P("strip", "sub"), P("strip", "sub"), P("strip", "sub"), P(None, "sub"), P()),
        out_specs=(P("strip", "sub"), P(("strip", "sub"))),
        check_vma=False,
    )
```

time: 516 us -> 81.8 us (0.16); the launches traced: 507 us -> 81.7 us
  blocking collectives: 234 us -> 0 us
  other arithmetic: 83.9 us -> 0 us
  Pallas kernels: 0 us -> 78.3 us
  starting transfers between devices: 71.9 us -> 0 us
  waiting for transfers between devices: 56.1 us -> 0 us
  local copies, waits for them, and re-layouts: 40.5 us -> 2.78 us
  between operations: 20.5 us -> 0.65 us
    psum x28 -> x0, blocking collectives: 234 us -> none  [one_axis_at_a_time(): return functools.reduce(lax.psum, axes, array)]
    pallas_call x0 -> x1, Pallas kernels: none -> 78.3 us  [body(): pl.pallas_call(lambda *refs: kernel((strips, subs), *refs), out_shape=(ja...]
    ppermute x36 -> x0, starting transfers between devices: 71.9 us -> none  [the longest x16 38.9 us: padded_2(): lax.ppermute(lax.slice_in_dim(block, block.shape[dim] - width, None, axis...]
    ppermute x36 -> x0, waiting for transfers between devices: 56.1 us -> none  [the longest x16 53.3 us: padded_2(): lax.ppermute(lax.slice_in_dim(block, 0, width, axis=dim), axis, backward)]
    mul x8 -> x0, other arithmetic: 34.8 us -> none  [wide_apply(): ((kappa_wide + 4.0) * padded[1:-1, 1:-1] - neighbours(padded)) * inside]
    concatenate x9 -> x0, local copies, waits for them, and re-layouts: 22.1 us -> none  [the longest x8 20.2 us: padded_2(): block = jnp.concatenate([low, block, high], axis=dim)]
    reduce_sum x9 -> x0, other arithmetic: 19.4 us -> none  [the longest x6 14.9 us: paired(): jnp.sum(residual * image)]
    sub x6 -> x0, other arithmetic: 10.3 us -> none  [the longest x4 6.96 us: joined_solve(): residual = residual - alpha * along]
  transfers between devices with their start and end apart: 36 -> 0, of which waited for: 19 -> 0; matrix products, arithmetic and copies ran while one was open for 3% -> 0% of each run, Pallas kernels for 0% -> 0%
where the time goes in v1:
time: 81.8 us; the launch traced here: 81.7 us
  Pallas kernels  78.3 us (96%)
  local copies, waits for them, and re-layouts  2.78 us (3%)
    pallas_call x1, Pallas kernels, body(): pl.pallas_call(lambda *refs: kernel((strips, subs), *refs), out_shape=(ja...  78.3 us
    unnamed x4, local copies, waits for them, and re-layouts  2.78 us

profile of v1, /device:TPU:0, one launch (start us, length us, event | category | flops | bytes accessed | tf_op | source)
XLA Modules:
  0.0 81.7 jit_solution(10217148066397895890)
XLA Ops:
  0.6 78.3 %shard_map.68 = (f32[32,8192]{1,0:T(8,128)}, f32[1,15]{1,0:T(1,128)}) custom-call(s32[32,8192]{1,0:T(8,128)} %refs_0_.1, f32[32,8192]{1,0:T(8,128)} %refs_1_.1, f32[32,8192]{1,0:T(8,128)} %refs_2_.1, s32[8,64]{1,0:T(8,128)} %refs_3_.1, s32[8,128]{1,0:T(8,128)} %bitcast.2), custom_call_target="tpu_custom_call" | custom-call | tf_op jit(solution)/shard_map/pallas_call | solution.py:631
  78.9 0.0 copy-start
  78.9 2.3 %copy.9 = f32[32,8192]{1,0:T(8,128)} copy(f32[32,8192]{1,0:T(8,128)} %get-tuple-element.8) | data formatting | bytes 2097152
  81.2 0.0 copy-done
  81.2 0.5 copy.10
Async XLA Ops:
  78.9 2.3 %copy-start = (f32[1,15]{1,0:T(1,128)S(1)}, f32[1,15]{1,0:T(1,128)}, u32[]{:S(2)}) copy-start(f32[1,15]{1,0:T(1,128)} %get-tuple-element.5) | copy-start | bytes 184

commit v2 on v0

v2 whole, which is shorter than its diff:
```python
import jax
import jax.numpy as jnp
from jax import lax
from jax.experimental import pallas as pl
from jax.experimental.pallas import tpu as pltpu
from jax.sharding import PartitionSpec as P

TILE = 128
OWNED_MOST = 15
MESH = pl.DeviceIdType.MESH
F32 = jnp.float32

ROWS, TOP, BOTTOM, SLOTS, DEEP = 32, 8, 40, 48, 5
PITCH = 80
OWN = tuple(range(8, 72, 8))
ALL = (1,) + OWN + (71,)
SHIFT = 20.0
SIGMA = (1.0, 2.0**-27)
TINY = 3e-7


def kernel(
    dims, counts_h, offset_h, kappa_h, labels_h, owner_h, mode_h, owned_ref,
    st_c, st_o, st_k, off_m, cnt_m, kap_m, w_m, r_m, t_m, a_m, b_m, q_m, mode_m,
    pack, land, edge, lab, own, pick, src1, src2, got1, got2,
    ld_sem, small_sem, row_s, row_r, edge_s, edge_r, lab_s, lab_r, s1, r1, s2, r2, out_sem,
):
    strips, subs = dims
    strip, sub = lax.axis_index("strip"), lax.axis_index("sub")
    core, chip = lax.rem(strip, 2), lax.div(strip, 2)
    chips, near = strips // 2, 2 * subs
    me1 = core * subs + sub
    up, down = lax.rem(strip + strips - 1, strips), lax.rem(strip + 1, strips)
    left, right = lax.rem(sub + subs - 1, subs), lax.rem(sub + 1, subs)
    first, last = strip == 0, strip == strips - 1

    def far(n, size):
        return min(n, size - n)

    peers1 = []
    for flip, dz in sorted(
        ((f, d) for f in range(2) for d in range(subs) if f or d),
        key=lambda v: (-far(v[1], subs), -v[0]),
    ):
        other, z = (1 - core if flip else core), lax.rem(sub + dz, subs)
        peers1.append((other * subs + z, (chip * 2 + other, z)))
    side = 4 if chips == 16 else 2
    tall = chips // side
    peers2 = []
    for dy, dx in sorted(
        ((y, x) for y in range(tall) for x in range(side) if y or x),
        key=lambda v: -far(v[0], tall) - far(v[1], side),
    ):
        j = lax.rem(lax.div(chip, side) + dy, tall) * side + lax.rem(lax.rem(chip, side) + dx, side)
        peers2.append((j, (j * 2 + core, sub)))

    def each(low, high, do):
        def step(k, carry):
            do(k)
            return carry

        lax.fori_loop(low, high, step, 0)

    barrier = pltpu.get_barrier_semaphore()
    around = [
        (up, sub), (down, sub), (strip, left), (strip, right),
        (up, left), (down, left), (up, right), (down, right),
    ]
    greeted = [device for _, device in peers2 + peers1] + around
    for device in greeted:
        pl.semaphore_signal(barrier, inc=1, device_id=device, device_id_type=MESH)

    order = (0, 3, 1, 2)
    loads = {}
    for i in order:
        for n, (hbm, stage) in enumerate(((offset_h, st_o), (counts_h, st_c), (kappa_h, st_k))):
            part = pl.ds(512 * i, 512)
            loads[i, n] = pltpu.make_async_copy(hbm.at[part, :], stage.at[part, :], ld_sem.at[3 * i + n])
            loads[i, n].start()
    load_owner = pltpu.make_async_copy(owner_h, own, small_sem.at[0])
    load_owner.start()
    load_labels = pltpu.make_async_copy(labels_h, lab.at[sub], small_sem.at[1])
    load_labels.start()

    lane = lax.broadcasted_iota(jnp.int32, (8, 128), 1)
    sublane = lax.broadcasted_iota(jnp.int32, (8, 128), 0)
    low_half = lane < 64
    zero = jnp.zeros((8, 128), F32)

    def relayout(i, wait=True):
        for n in range(3 if wait else 0):
            loads[i, n].wait()

        def pair(m):
            row = 2 * m

            def turned(stage):
                x = [
                    [
                        stage[pl.ds(512 * i + 64 * g + row + d, 8, stride=8), :].astype(F32)
                        for g in range(8)
                    ]
                    for d in range(2)
                ]
                upper = [jnp.where(low_half, x[0][g], pltpu.roll(x[1][g], 64, axis=1)) for g in range(8)]
                lower = [jnp.where(low_half, pltpu.roll(x[0][g], 64, axis=1), x[1][g]) for g in range(8)]
                return jnp.concatenate(upper + lower, axis=0).T

            off, cnt, kap = turned(st_o), turned(st_c), turned(st_k)
            for d in range(2):
                q = TOP + 8 * i + row + d
                part = slice(64 * d, 64 * d + 64)
                weight = jnp.exp(off[part])
                off_m[q, 8:72, :] = off[part]
                cnt_m[q, 8:72, :] = cnt[part]
                kap_m[q, 8:72, :] = kap[part] + 4.0
                w_m[q, 8:72, :] = 10.0 * weight
                r_m[q, 8:72, :] = cnt[part] - weight

        each(0, 4, pair)

    def remote(src, dst, send, recv, device):
        return pltpu.make_async_remote_copy(
            src_ref=src, dst_ref=dst, send_sem=send, recv_sem=recv,
            device_id=device, device_id_type=MESH,
        )

    def row_copies(field, n, low, high):
        many = high - low

        def rows(q):
            return field.at[pl.ds(q, many), pl.ds(8, 64), :]

        return [
            remote(rows(TOP + low), rows(BOTTOM + low), row_s.at[2 * n], row_r.at[2 * n], (up, sub)),
            remote(
                rows(BOTTOM - high), rows(TOP - high),
                row_s.at[2 * n + 1], row_r.at[2 * n + 1], (down, sub),
            ),
        ]

    def edge_copies(n):
        made = []
        for to, beside in ((1, left), (0, right)):
            for m, device in enumerate(((strip, beside), (down, beside), (up, beside))):
                k = 6 * n + 3 * to + m
                made.append(
                    remote(pack.at[n, to], land.at[k], edge_s.at[k], edge_r.at[k], device)
                )
        return made

    def pack_field(field, n):
        tiles = [zero, zero]
        for q in range(TOP, BOTTOM):
            for to, p, l in ((1, 8, 0), (0, 64, 127)):
                moved = pltpu.roll(field[q, p : p + 8, :], (q - l) % 128, axis=1)
                tiles[to] = jnp.where(lane == q, moved, tiles[to])
        for to in range(2):
            pack[n, to] = tiles[to]

    def pack_stage(stage, n):
        for to, g, keep in ((1, 0, slice(0, 8)), (0, 63, slice(120, 128))):
            x = [stage[pl.ds(512 * i + 8 * g, 8), :].astype(F32) for i in range(4)]
            pack[n, to] = jnp.concatenate([zero] + x + [zero] * 11, axis=0).T[keep]

    def landed(n, to):
        k = 6 * n + 3 * to
        return jnp.where(
            lane < TOP, pltpu.roll(land[k + 1], 96, axis=1),
            jnp.where(lane < BOTTOM, land[k], pltpu.roll(land[k + 2], 32, axis=1)),
        )

    def start(copies):
        for copy in copies:
            copy.start()

    def arrived(copies):
        for copy in copies:
            copy.wait_recv()

    def sent(copies):
        for copy in copies:
            copy.wait_send()

    left_open = jnp.where(sub > 0, 1.0, 0.0).astype(F32)
    right_open = jnp.where(sub < subs - 1, 1.0, 0.0).astype(F32)
    left_shut = jnp.where((lane == 0) & (sublane < 7), 1.0 - left_open, 0.0) > 0.5
    right_shut = jnp.where((lane == 127) & (sublane >= 1), 1.0 - right_open, 0.0) > 0.5

    def at(field, q, p):
        return field[q, p : p + 8, :]

    def put(field, q, p, value):
        field[q, p : p + 8, :] = value

    def k_tile(field, q, p, many):
        window = [at(field, q - 1 + m, p) for m in range(many + 2)]
        made = []
        for m in range(many):
            beside = at(field, q + m, p - 1) + at(field, q + m, p + 1)
            value = at(kap_m, q + m, p) * window[m + 1] - ((window[m] + window[m + 2]) + beside)
            if p == ALL[0]:
                value = jnp.where(left_shut, 0.0, value)
            if p == ALL[-1]:
                value = jnp.where(right_shut, 0.0, value)
            made.append(value)
        return made, window[1:-1]

    def blank(field, low, high):
        nothing = jnp.zeros((PITCH, 128), F32)

        @pl.when(first)
        def _():
            for q in range(low, TOP):
                field[q] = nothing

        @pl.when(last)
        def _():
            for q in range(BOTTOM, high):
                field[q] = nothing

    def blocks(low, high, many, do):
        each(0, (high - low) // many, lambda n: do(low + many * n))

    def apply_k(field, out, low, high, many):
        def block(q):
            for p in ALL:
                made, _ = k_tile(field, q, p, many)
                for m in range(many):
                    put(out, q + m, p, made[m])

        blocks(low, high, many, block)
        blank(out, low, high)

    def shifted(base, out, low, high, shift, sigma, products):
        def block(q, many, carry):
            for p in ALL:
                made, _ = k_tile(t_m, q, p, many)
                for m in range(many):
                    value, weight = at(base, q + m, p), at(w_m, q + m, p)
                    if shift:
                        weight = weight - sigma * shift
                    got = (made[m] if sigma == 1.0 else sigma * made[m]) + weight * value
                    put(out, q + m, p, got)
                    if carry is not None and p in OWN:
                        terms = products(q + m, p, value, got)
                        h = (p // 8) % 2
                        carry[h] = [c + x for c, x in zip(carry[h], terms)]
            return carry

        each(low, TOP, lambda q: block(q, 1, None) and None)
        each(BOTTOM, high, lambda q: block(q, 1, None) and None)
        count = len(products(TOP, 8, zero, zero))

        def some(n, carry):
            got = block(TOP + 2 * n, 2, [list(carry[:count]), list(carry[count:])])
            return tuple(got[0] + got[1])

        total = lax.fori_loop(0, ROWS // 2, some, (zero,) * (2 * count))
        blank(out, low, high)
        return [total[k] + total[count + k] for k in range(count)]

    def inject(field, edges):
        for q in range(TOP - DEEP, BOTTOM + DEEP):
            x = at(field, q, 64)
            ghost = jnp.where(low_half, pltpu.roll(x, 65, axis=1), pltpu.roll(x, 64, axis=1))
            put(field, q, 0, jnp.where(lane == 0, pltpu.roll(edges[0], (128 - q) % 128, axis=1), ghost))
            x = at(field, q, 8)
            ghost = jnp.where(low_half, pltpu.roll(x, 64, axis=1), pltpu.roll(x, 63, axis=1))
            put(field, q, 72, jnp.where(lane == 127, pltpu.roll(edges[1], 127 - q, axis=1), ghost))

    def hop(peers, src, got, send, recv, size, mine, u):
        for m, (_, device) in enumerate(peers):
            remote(src.at[u], got.at[size * u + mine], send.at[size * u + m], recv.at[size * u + mine], device).start()

    def hop_done(peers, src, got, send, recv, size, u):
        for m, (slot, device) in enumerate(peers):
            remote(src.at[u], got.at[size * u + slot], send.at[size * u + m], recv.at[size * u + slot], device).wait()

    def hop1(u, message):
        src1[u] = message
        got1[near * u + me1] = message
        hop(peers1, src1, got1, s1, r1, near, me1, u)

    def hop2(u, message):
        src2[u] = message
        got2[chips * u + chip] = message
        hop(peers2, src2, got2, s2, r2, chips, chip, u)

    def added(terms):
        while len(terms) > 1:
            terms = [a + b for a, b in zip(terms[::2], terms[1::2])] + terms[len(terms) // 2 * 2 :]
        return terms[0]

    def over_sublanes(v):
        for n in (4, 2, 1):
            v = v + pltpu.roll(v, n, axis=0)
        return v

    def moments_out(u, sums):
        message = zero
        for n, v in enumerate(sums):
            message = jnp.where(sublane == n, over_sublanes(v), message)
        hop1(u, message)

    def moments_on(u):
        hop_done(peers1, src1, got1, s1, r1, near, u)
        total = added([got1[near * u + j] for j in range(near)])
        hop2(u, jnp.concatenate([total, zero], axis=0))

    def moments_in(u):
        hop_done(peers2, src2, got2, s2, r2, chips, u)
        total = added([got2[chips * u + j, 0:8, :] for j in range(chips)])
        flat = jnp.sum(total, axis=1, keepdims=True)
        return [jnp.broadcast_to(flat[n : n + 1, :], (8, 128)) for n in range(6)]

    def solve(moments, sigma):
        g00, g01, g11, g12, g22, h22 = moments
        inverse = 1.0 / sigma
        a00 = inverse * g01
        a01 = inverse * g11
        a02 = inverse * g12
        a11 = a02 + SHIFT * g11
        a12 = inverse * g22 + SHIFT * g12
        a22 = inverse * h22
        i0 = 1.0 / a00
        l10, l20 = a01 * i0, a02 * i0
        d1, u12 = a11 - l10 * a01, a12 - l10 * a02
        i1 = jnp.where(d1 > TINY * a11, 1.0 / d1, 0.0)
        l21 = u12 * i1
        d2 = a22 - l20 * a02 - l21 * u12
        i2 = jnp.where(d2 > TINY * a22, 1.0 / d2, 0.0)
        y0 = 10.0 * g00
        y1 = 10.0 * g01 - l10 * y0
        y2 = 10.0 * (g11 - (sigma * SHIFT) * g01) - l20 * y0 - l21 * y1
        c2 = y2 * i2
        c1 = y1 * i1 - l21 * c2
        c0 = y0 * i0 - l10 * c1 - l20 * c2
        return c0, c1, c2

    relayout(order[0])
    relayout(order[1])
    for i in (1, 2):
        for n in range(3):
            loads[i, n].wait()
    for n, stage in enumerate((st_o, st_c, st_k)):
        pack_stage(stage, n)
    pl.semaphore_wait(barrier, len(greeted))
    halo = []
    for n in range(3):
        halo += edge_copies(n)
    halo += row_copies(off_m, 0, 0, 5) + row_copies(cnt_m, 1, 0, 5) + row_copies(kap_m, 2, 0, 4)
    start(halo)
    load_labels.wait()

    def label_copy(k, arriving):
        z = lax.rem(sub + k, subs)
        held = z if arriving else sub
        return remote(labels_h, lab.at[held], lab_s.at[k], lab_r.at[held], (strip, z))

    for k in range(1, subs):
        label_copy(k, False).start()
    relayout(order[2], False)
    relayout(order[3], False)
    arrived(halo)

    def halo_rows(do):
        each(TOP - DEEP, TOP, do)
        each(BOTTOM, BOTTOM + DEEP, do)

    def prime(q):
        for p in OWN:
            weight = jnp.exp(at(off_m, q, p))
            put(w_m, q, p, 10.0 * weight)
            put(r_m, q, p, at(cnt_m, q, p) - weight)

    halo_rows(prime)
    alive = (left_open, right_open)
    e_off = [landed(0, to) for to in range(2)]
    e_cnt = [landed(1, to) for to in range(2)]
    e_kap = [landed(2, to) + 4.0 for to in range(2)]
    e_w = [jnp.exp(v) for v in e_off]
    e_r = [(cnt - weight) * live for cnt, weight, live in zip(e_cnt, e_w, alive)]
    e_w = [10.0 * v for v in e_w]
    inject(kap_m, e_kap)
    inject(w_m, e_w)
    inject(r_m, e_r)
    blank(r_m, TOP - DEEP, BOTTOM + DEEP)
    for to in range(2):
        for n, v in enumerate((e_off[to], e_cnt[to], e_w[to], e_r[to])):
            edge[2 * n + to] = v

    def basis(n):
        sigma = SIGMA[n]
        apply_k(r_m, t_m, 4, 44, 4)
        g00, g01, g11 = shifted(
            r_m, a_m, 5, 43, 0.0, sigma, lambda q, p, r, a: (r * r, r * a, a * a)
        )
        moving = []
        if n == 0:
            pack_field(a_m, 3)
            moving = edge_copies(3) + row_copies(a_m, 3, 3, 5)
            start(moving)
        apply_k(a_m, t_m, 6, 42, 4)
        g12, g22 = shifted(a_m, b_m, 7, 41, SHIFT, sigma, lambda q, p, a, b: (a * b, b * b))
        if n == 0:
            pack_field(b_m, 4)
            more = edge_copies(4) + row_copies(b_m, 4, 1, 5)
            start(more)
            moving = moving + more

        def energy(m, carry):
            carry = list(carry)
            q = TOP + 4 * m
            for p in OWN:
                made, values = k_tile(b_m, q, p, 4)
                for k in range(4):
                    square = made[k] * made[k]
                    carry[k % 2] = carry[k % 2] + (
                        (square if sigma == 1.0 else sigma * square)
                        + at(w_m, q + k, p) * (values[k] * values[k])
                    )
            return tuple(carry)

        h22 = added(list(lax.fori_loop(0, ROWS // 4, energy, (zero, zero))))
        moments_out(n, (g00, g01, g11, g12, g22, h22))
        return moving

    moving = basis(0)
    moments_on(0)

    arrived(moving)
    e_a = [landed(3, to) for to in range(2)]
    e_b = [landed(4, to) for to in range(2)]
    inject(b_m, [v * live for v, live in zip(e_b, alive)])
    blank(b_m, TOP - DEEP, BOTTOM + DEEP)
    apply_k(b_m, t_m, 7, 41, 2)

    def second_k(q):
        for p in OWN:
            made, _ = k_tile(t_m, q, p, 4)
            for m in range(4):
                put(q_m, q + m, p, made[m])

    blocks(TOP, BOTTOM, 4, second_k)
    pack_field(q_m, 5)
    final = edge_copies(5) + row_copies(q_m, 5, 0, 5)
    start(final)
    sent(moving)

    c0, c1, c2 = solve(moments_in(0), SIGMA[0])
    d0, d1, d2 = 0.1 * c0, 0.1 * c1, 0.1 * c2

    def renew(off, cnt, weight, r, a, b, qb):
        step = c0 * r + (c1 * a + c2 * b)
        q_mode = d0 * (a - weight * r) + (d1 * (b + (SHIFT - weight) * a) + d2 * qb)
        fresh = jnp.exp(off + step)
        return step, (10.0 * SIGMA[1]) * fresh, cnt - fresh - q_mode

    def renew_row(q, keep):
        for p in OWN:
            step, fresh, gradient = renew(*(at(f, q, p) for f in (off_m, cnt_m, w_m, r_m, a_m, b_m, q_m)))
            if keep:
                put(mode_m, q, p, step)
            put(w_m, q, p, fresh)
            put(r_m, q, p, gradient)

    each(TOP, BOTTOM, lambda q: renew_row(q, True))
    arrived(final)
    halo_rows(lambda q: renew_row(q, False))
    e_w, e_r = [], []
    for to in range(2):
        _, fresh, gradient = renew(
            edge[to], edge[2 + to], edge[4 + to], edge[6 + to], e_a[to], e_b[to], landed(5, to)
        )
        e_w.append(fresh)
        e_r.append(gradient * alive[to])
    inject(w_m, e_w)
    inject(r_m, e_r)
    blank(r_m, TOP - DEEP, BOTTOM + DEEP)

    basis(1)
    moments_on(1)

    sent(final)
    sent(halo)
    for k in range(1, subs):
        label_copy(k, True).wait()
    load_owner.wait()
    myself = strip * subs + sub
    mark = jnp.where(own[...] == myself, 1, 0)
    count = mark
    for n in (1, 2, 4, 8, 16, 32, 64):
        count = count + jnp.where(lane >= n, pltpu.roll(count, n, axis=1), 0)
    whole = jnp.broadcast_to(count[:, 127:128], (8, 128))
    below = jnp.where(sublane >= 1, pltpu.roll(whole, 1, axis=0), 0)
    for n in (1, 2, 4):
        below = below + jnp.where(sublane >= n, pltpu.roll(below, n, axis=0), 0)
    slot = jnp.where(mark == 1, count + below - 1, -1)
    region = (sublane * 128 + lane).astype(F32)
    tiles = [
        jnp.concatenate([lab[2 * h], lab[2 * h + 1]], axis=1).astype(F32) for h in range(2)
    ]
    for s in range(OWNED_MOST):
        mine = jnp.max(jnp.where(slot == s, region, -1.0), axis=1, keepdims=True)
        mine = jnp.max(mine, axis=0, keepdims=True)
        for h in range(2):
            pick[s, pl.ds(8 * h, 8), :] = jnp.where(tiles[h] == mine, 1.0, 0.0)

    c0, c1, c2 = solve(moments_in(1), SIGMA[1])

    def finish(q, carry):
        sums = list(carry)
        for p in OWN:
            mode = at(mode_m, q, p) + (c0 * at(r_m, q, p) + (c1 * at(a_m, q, p) + c2 * at(b_m, q, p)))
            put(mode_m, q, p, mode)
            h = (p // 8) % 4
            sums[h] = sums[h] + jnp.exp(at(off_m, q, p) + mode)
        return tuple(sums)

    line = over_sublanes(added(list(lax.fori_loop(TOP, BOTTOM, finish, (zero,) * 4))))
    line = line + pltpu.roll(line, 64, axis=1)
    mine = (sublane == lax.div(strip, TILE // ROWS)) & (lax.div(lane, 64) == lax.rem(sub, 2))
    hop1(2, jnp.where(mine, line * (1.0 / (TILE * TILE)), 0.0))

    outs = []

    def write_out(i):
        def pair(m):
            row = 2 * m
            q = TOP + 8 * i + row
            x = jnp.concatenate([mode_m[q, 8:72, :], mode_m[q + 1, 8:72, :]], axis=0).T
            for g in range(8):
                upper, lower = x[8 * g : 8 * g + 8], x[64 + 8 * g : 72 + 8 * g]
                to = 512 * i + 64 * g + row
                st_o[pl.ds(to, 8, stride=8), :] = jnp.where(low_half, upper, pltpu.roll(lower, 64, axis=1))
                st_o[pl.ds(to + 1, 8, stride=8), :] = jnp.where(low_half, pltpu.roll(upper, 64, axis=1), lower)

        each(0, 4, pair)
        part = pl.ds(512 * i, 512)
        outs.append(pltpu.make_async_copy(st_o.at[part, :], mode_h.at[part, :], out_sem.at[i]))
        outs[-1].start()

    write_out(0)
    write_out(1)
    hop_done(peers1, src1, got1, s1, r1, near, 2)
    both = []
    for h in range(2):
        slots = [c * subs + z for c in range(2) for z in (2 * h, 2 * h + 1)]
        both.append(added([got1[near * 2 + j] for j in slots]))
    hop2(2, jnp.concatenate(both, axis=0))
    write_out(2)
    write_out(3)
    hop_done(peers2, src2, got2, s2, r2, chips, 2)
    total = added([got2[chips * 2 + j] for j in range(chips)])
    answer = zero
    for h in range(2):
        gathered = zero
        for s in range(8 * h, min(8 * h + 8, OWNED_MOST)):
            both = total * pick[s]
            gathered = jnp.where(
                sublane == s - 8 * h, over_sublanes(both[0:8] + both[8:16]), gathered
            )
        flat = jnp.sum(gathered, axis=1, keepdims=True)
        answer = answer + jnp.where(lane == sublane + 8 * h, flat, 0.0)
    owned_ref[...] = over_sublanes(answer)[0:1, 0:OWNED_MOST]
    for copy in outs:
        copy.wait()


def solution(mesh):
    strips, subs = mesh.shape["strip"], mesh.shape["sub"]
    near, chips = 2 * subs, strips // 2

    def tiled(x):
        return x.reshape(4, 8, 64, 128).transpose(0, 2, 1, 3).reshape(2048, 128)

    def body(counts, offset, kappa, labels, owner):
        field = pltpu.VMEM((SLOTS, PITCH, 128), F32)
        stage = pltpu.VMEM((2048, 128), F32)
        dma = pltpu.SemaphoreType.DMA
        anywhere = pl.BlockSpec(memory_space=pl.ANY)
        mode, owned = pl.pallas_call(
            lambda *refs: kernel((strips, subs), *refs),
            out_shape=(
                jax.ShapeDtypeStruct((2048, 128), F32),
                jax.ShapeDtypeStruct((1, OWNED_MOST), F32),
            ),
            in_specs=[anywhere] * 5,
            out_specs=(anywhere, pl.BlockSpec(memory_space=pltpu.VMEM)),
            scratch_shapes=[
                pltpu.VMEM((2048, 128), jnp.int32), stage, stage,
                field, field, field, field, field, field, field, field, field, field,
                pltpu.VMEM((6, 2, 8, 128), F32),
                pltpu.VMEM((36, 8, 128), F32),
                pltpu.VMEM((8, 8, 128), F32),
                pltpu.VMEM((subs, 8, labels.shape[1]), jnp.int32),
                pltpu.VMEM((8, 128), jnp.int32),
                pltpu.VMEM((OWNED_MOST, 16, 128), F32),
                pltpu.VMEM((3, 8, 128), F32),
                pltpu.VMEM((3, 16, 128), F32),
                pltpu.VMEM((3 * near, 8, 128), F32),
                pltpu.VMEM((3 * chips, 16, 128), F32),
                dma((12,)), dma((2,)), dma((12,)), dma((12,)), dma((36,)), dma((36,)),
                dma((subs,)), dma((subs,)), dma((3 * near,)), dma((3 * near,)),
                dma((3 * chips,)), dma((3 * chips,)), dma((4,)),
            ],
            compiler_params=pltpu.CompilerParams(
                collective_id=0, has_side_effects=True, vmem_limit_bytes=63 << 20
            ),
        )(tiled(counts), tiled(offset), tiled(kappa), labels, owner.reshape(8, 128))
        mode = mode.reshape(4, 64, 8, 128).transpose(0, 2, 1, 3).reshape(32, 8192)
        return mode, owned.reshape(OWNED_MOST)

    return jax.shard_map(
        body,
        mesh=mesh,
        in_specs=(P("strip", "sub"), P("strip", "sub"), P("strip", "sub"), P(None, "sub"), P()),
        out_specs=(P("strip", "sub"), P(("strip", "sub"))),
        check_vma=False,
    )
```

time: 516 us -> 60.8 us (0.12); the launches traced: 507 us -> 60.7 us
  blocking collectives: 234 us -> 0 us
  other arithmetic: 83.9 us -> 0 us
  starting transfers between devices: 71.9 us -> 0 us
  Pallas kernels: 0 us -> 57.2 us
  waiting for transfers between devices: 56.1 us -> 0 us
  local copies, waits for them, and re-layouts: 40.5 us -> 2.78 us
  between operations: 20.5 us -> 0.65 us
    psum x28 -> x0, blocking collectives: 234 us -> none  [one_axis_at_a_time(): return functools.reduce(lax.psum, axes, array)]
    ppermute x36 -> x0, starting transfers between devices: 71.9 us -> none  [the longest x16 38.9 us: padded_2(): lax.ppermute(lax.slice_in_dim(block, block.shape[dim] - width, None, axis...]
    pallas_call x0 -> x1, Pallas kernels: none -> 57.2 us  [body(): pl.pallas_call(lambda *refs: kernel((strips, subs), *refs), out_shape=(ja...]
    ppermute x36 -> x0, waiting for transfers between devices: 56.1 us -> none  [the longest x16 53.3 us: padded_2(): lax.ppermute(lax.slice_in_dim(block, 0, width, axis=dim), axis, backward)]
    mul x8 -> x0, other arithmetic: 34.8 us -> none  [wide_apply(): ((kappa_wide + 4.0) * padded[1:-1, 1:-1] - neighbours(padded)) * inside]
    concatenate x9 -> x0, local copies, waits for them, and re-layouts: 22.1 us -> none  [the longest x8 20.2 us: padded_2(): block = jnp.concatenate([low, block, high], axis=dim)]
    reduce_sum x9 -> x0, other arithmetic: 19.4 us -> none  [the longest x6 14.9 us: paired(): jnp.sum(residual * image)]
    sub x6 -> x0, other arithmetic: 10.3 us -> none  [the longest x4 6.96 us: joined_solve(): residual = residual - alpha * along]
  transfers between devices with their start and end apart: 36 -> 0, of which waited for: 19 -> 0; matrix products, arithmetic and copies ran while one was open for 3% -> 0% of each run, Pallas kernels for 0% -> 0%
where the time goes in v2:
time: 60.8 us; the launch traced here: 60.7 us
  Pallas kernels  57.2 us (94%)
  local copies, waits for them, and re-layouts  2.78 us (5%)
  between operations  0.65 us (1%)
    pallas_call x1, Pallas kernels, body(): pl.pallas_call(lambda *refs: kernel((strips, subs), *refs), out_shape=(ja...  57.2 us
    unnamed x4, local copies, waits for them, and re-layouts  2.78 us

profile of v2, /device:TPU:0, one launch (start us, length us, event | category | flops | bytes accessed | tf_op | source)
XLA Modules:
  0.0 60.7 jit_solution(13537066187920437025)
XLA Ops:
  0.6 57.2 %shard_map.68 = (f32[2048,128]{1,0:T(8,128)}, f32[1,15]{1,0:T(1,128)}) custom-call(s32[2048,128]{1,0:T(8,128)} %bitcast.22, f32[2048,128]{1,0:T(8,128)} %bitcast.23, f32[2048,128]{1,0:T(8,128)} %bitcast.24, s32[8,64]{1,0:T(8,128)} %refs_3_.1, s32[8,128]{1,0:T(8,128)} %bitcast.26), custom_call_target="tpu_custom_call" | custom-call | tf_op jit(solution)/shard_map/pallas_call | solution.py:583
  57.9 0.0 copy-start
  57.9 2.3 %copy.9 = f32[32,8192]{1,0:T(8,128)} copy(f32[32,8192]{1,0:T(8,128)} %bitcast.25) | data formatting | bytes 2097152
  60.1 0.0 copy-done
  60.1 0.5 copy.10
Async XLA Ops:
  57.9 2.3 %copy-start = (f32[1,15]{1,0:T(1,128)S(1)}, f32[1,15]{1,0:T(1,128)}, u32[]{:S(2)}) copy-start(f32[1,15]{1,0:T(1,128)} %get-tuple-element.5) | copy-start | bytes 184

commit v3 on v2

--- a/solution.py
+++ b/solution.py
@@ -14,15 +14,15 @@
 PITCH = 80
 OWN = tuple(range(8, 72, 8))
 ALL = (1,) + OWN + (71,)
-SHIFT = 20.0
+SHIFTS = (3.0, 40.0)
 SIGMA = (1.0, 2.0**-27)
 TINY = 3e-7
 
 
 def kernel(
     dims, counts_h, offset_h, kappa_h, labels_h, owner_h, mode_h, owned_ref,
-    st_c, st_o, st_k, off_m, cnt_m, kap_m, w_m, r_m, t_m, a_m, b_m, q_m, mode_m,
-    pack, land, edge, lab, own, pick, src1, src2, got1, got2,
+    st_c, st_o, st_k, off_m, kap_m, w_m, r_m, t_m, a_m, b_m, q_m, mode_m,
+    pack, land, lab, own, pick, src1, src2, got1, got2,
     ld_sem, small_sem, row_s, row_r, edge_s, edge_r, lab_s, lab_r, s1, r1, s2, r2, out_sem,
 ):
     strips, subs = dims
@@ -112,7 +112,6 @@
                 part = slice(64 * d, 64 * d + 64)
                 weight = jnp.exp(off[part])
                 off_m[q, 8:72, :] = off[part]
-                cnt_m[q, 8:72, :] = cnt[part]
                 kap_m[q, 8:72, :] = kap[part] + 4.0
                 w_m[q, 8:72, :] = 10.0 * weight
                 r_m[q, 8:72, :] = cnt[part] - weight
@@ -158,10 +157,15 @@
         for to in range(2):
             pack[n, to] = tiles[to]
 
-    def pack_stage(stage, n):
+    def pack_inputs():
         for to, g, keep in ((1, 0, slice(0, 8)), (0, 63, slice(120, 128))):
-            x = [stage[pl.ds(512 * i + 8 * g, 8), :].astype(F32) for i in range(4)]
-            pack[n, to] = jnp.concatenate([zero] + x + [zero] * 11, axis=0).T[keep]
+            tiles = []
+            for stage in (st_o, st_c, st_k):
+                x = [stage[pl.ds(512 * i + 8 * g, 8), :].astype(F32) for i in range(4)]
+                tiles.append(jnp.concatenate([zero] + x + [zero] * 11, axis=0).T[keep])
+            pack[0, to] = tiles[0]
+            pack[1, to] = tiles[1] - jnp.exp(tiles[0])
+            pack[2, to] = tiles[2]
 
     def landed(n, to):
         k = 6 * n + 3 * to
@@ -222,46 +226,47 @@
     def blocks(low, high, many, do):
         each(0, (high - low) // many, lambda n: do(low + many * n))
 
+    def k_block(field, out, q, many):
+        for p in ALL:
+            made, _ = k_tile(field, q, p, many)
+            for m in range(many):
+                put(out, q + m, p, made[m])
+
     def apply_k(field, out, low, high, many):
-        def block(q):
-            for p in ALL:
-                made, _ = k_tile(field, q, p, many)
-                for m in range(many):
-                    put(out, q + m, p, made[m])
-
-        blocks(low, high, many, block)
-        blank(out, low, high)
-
-    def shifted(base, out, low, high, shift, sigma, products):
-        def block(q, many, carry):
-            for p in ALL:
-                made, _ = k_tile(t_m, q, p, many)
-                for m in range(many):
-                    value, weight = at(base, q + m, p), at(w_m, q + m, p)
-                    if shift:
-                        weight = weight - sigma * shift
-                    got = (made[m] if sigma == 1.0 else sigma * made[m]) + weight * value
-                    put(out, q + m, p, got)
-                    if carry is not None and p in OWN:
-                        terms = products(q + m, p, value, got)
-                        h = (p // 8) % 2
-                        carry[h] = [c + x for c, x in zip(carry[h], terms)]
-            return carry
-
-        each(low, TOP, lambda q: block(q, 1, None) and None)
-        each(BOTTOM, high, lambda q: block(q, 1, None) and None)
-        count = len(products(TOP, 8, zero, zero))
-
+        blocks(low, high, many, lambda q: k_block(field, out, q, many))
+
+    def summed(sums, n, terms):
+        sums[n % 2] = [x + y for x, y in zip(sums[n % 2], terms)]
+
+    def shift_block(base, out, q, many, shift, sigma, products, sums, counted):
+        for p in ALL:
+            made, _ = k_tile(t_m, q, p, many)
+            for m in range(many):
+                value, weight = at(base, q + m, p), at(w_m, q + m, p)
+                got = (made[m] if sigma == 1.0 else sigma * made[m]) + (weight - sigma * shift) * value
+                put(out, q + m, p, got)
+                if m in counted and p in OWN:
+                    summed(sums, m + p // 8, products(value, got))
+
+    def energy_block(q, many, sigma, sums):
+        for p in OWN:
+            made, values = k_tile(b_m, q, p, many)
+            for m in range(many):
+                square = made[m] * made[m]
+                square = square if sigma == 1.0 else sigma * square
+                summed(sums, m + p // 8, [square + at(w_m, q + m, p) * (values[m] * values[m])])
+
+    def sum_blocks(low, high, many, count, do):
         def some(n, carry):
-            got = block(TOP + 2 * n, 2, [list(carry[:count]), list(carry[count:])])
-            return tuple(got[0] + got[1])
-
-        total = lax.fori_loop(0, ROWS // 2, some, (zero,) * (2 * count))
-        blank(out, low, high)
-        return [total[k] + total[count + k] for k in range(count)]
-
-    def inject(field, edges):
-        for q in range(TOP - DEEP, BOTTOM + DEEP):
+            sums = [list(carry[:count]), list(carry[count:])]
+            do(low + many * n, sums)
+            return tuple(sums[0] + sums[1])
+
+        total = lax.fori_loop(0, (high - low) // many, some, (zero,) * (2 * count))
+        return [list(total[:count]), list(total[count:])]
+
+    def inject(field, edges, low, high):
+        for q in range(low, high):
             x = at(field, q, 64)
             ghost = jnp.where(low_half, pltpu.roll(x, 65, axis=1), pltpu.roll(x, 64, axis=1))
             put(field, q, 0, jnp.where(lane == 0, pltpu.roll(edges[0], (128 - q) % 128, axis=1), ghost))
@@ -269,23 +274,35 @@
             ghost = jnp.where(low_half, pltpu.roll(x, 64, axis=1), pltpu.roll(x, 63, axis=1))
             put(field, q, 72, jnp.where(lane == 127, pltpu.roll(edges[1], 127 - q, axis=1), ghost))
 
+    def inject_halo(field, edges, near_=0, far_=DEEP):
+        inject(field, edges, TOP - far_, TOP - near_)
+        inject(field, edges, BOTTOM + near_, BOTTOM + far_)
+
     def hop(peers, src, got, send, recv, size, mine, u):
         for m, (_, device) in enumerate(peers):
-            remote(src.at[u], got.at[size * u + mine], send.at[size * u + m], recv.at[size * u + mine], device).start()
+            remote(src.at[u], got.at[u, :, pl.ds(mine, 1), :], send.at[size * u + m], recv.at[size * u + mine], device).start()
 
     def hop_done(peers, src, got, send, recv, size, u):
         for m, (slot, device) in enumerate(peers):
-            remote(src.at[u], got.at[size * u + slot], send.at[size * u + m], recv.at[size * u + slot], device).wait()
-
-    def hop1(u, message):
-        src1[u] = message
-        got1[near * u + me1] = message
+            remote(src.at[u], got.at[u, :, pl.ds(slot, 1), :], send.at[size * u + m], recv.at[size * u + slot], device).wait()
+
+    def hop1(u, row):
+        src1[u, 0] = row
         hop(peers1, src1, got1, s1, r1, near, me1, u)
 
-    def hop2(u, message):
-        src2[u] = message
-        got2[chips * u + chip] = message
+    def hop1_in(u, row):
+        hop_done(peers1, src1, got1, s1, r1, near, u)
+        return jnp.where(sublane[0:near] == me1, row, got1[u, 0])
+
+    def hop2(u, rows):
+        for h in range(2):
+            src2[u, h] = rows[h]
         hop(peers2, src2, got2, s2, r2, chips, chip, u)
+
+    def hop2_in(u, rows):
+        hop_done(peers2, src2, got2, s2, r2, chips, u)
+        which = lax.broadcasted_iota(jnp.int32, (chips, 128), 0)
+        return [jnp.where(which == chip, rows[h], got2[u, h]) for h in range(2)]
 
     def added(terms):
         while len(terms) > 1:
@@ -301,27 +318,30 @@
         message = zero
         for n, v in enumerate(sums):
             message = jnp.where(sublane == n, over_sublanes(v), message)
-        hop1(u, message)
-
-    def moments_on(u):
-        hop_done(peers1, src1, got1, s1, r1, near, u)
-        total = added([got1[near * u + j] for j in range(near)])
-        hop2(u, jnp.concatenate([total, zero], axis=0))
-
-    def moments_in(u):
-        hop_done(peers2, src2, got2, s2, r2, chips, u)
-        total = added([got2[chips * u + j, 0:8, :] for j in range(chips)])
-        flat = jnp.sum(total, axis=1, keepdims=True)
-        return [jnp.broadcast_to(flat[n : n + 1, :], (8, 128)) for n in range(6)]
+        flat = jnp.sum(message, axis=1, keepdims=True)
+        row = over_sublanes(jnp.where(lane == sublane, flat, 0.0))[0:1]
+        hop1(u, row)
+        return row
+
+    def moments_on(u, row):
+        row = over_sublanes(hop1_in(u, row))[0:1]
+        hop2(u, [row, row])
+        return row
+
+    def moments_in(u, row):
+        total = over_sublanes(added([v for v in jnp.split(hop2_in(u, [row, row])[0], chips // 8)]))
+        return [jnp.broadcast_to(total[:, n : n + 1], (8, 128)) for n in range(6)]
 
     def solve(moments, sigma):
         g00, g01, g11, g12, g22, h22 = moments
         inverse = 1.0 / sigma
-        a00 = inverse * g01
-        a01 = inverse * g11
-        a02 = inverse * g12
-        a11 = a02 + SHIFT * g11
-        a12 = inverse * g22 + SHIFT * g12
+        t0, t1 = SHIFTS
+        g02 = g11 + (sigma * (t0 - t1)) * g01
+        a00 = inverse * g01 + t0 * g00
+        a01 = inverse * g11 + t0 * g01
+        a02 = inverse * g12 + t0 * g02
+        a11 = inverse * g12 + t1 * g11
+        a12 = inverse * g22 + t1 * g12
         a22 = inverse * h22
         i0 = 1.0 / a00
         l10, l20 = a01 * i0, a02 * i0
@@ -332,7 +352,7 @@
         i2 = jnp.where(d2 > TINY * a22, 1.0 / d2, 0.0)
         y0 = 10.0 * g00
         y1 = 10.0 * g01 - l10 * y0
-        y2 = 10.0 * (g11 - (sigma * SHIFT) * g01) - l20 * y0 - l21 * y1
+        y2 = 10.0 * g02 - l20 * y0 - l21 * y1
         c2 = y2 * i2
         c1 = y1 * i1 - l21 * c2
         c0 = y0 * i0 - l10 * c1 - l20 * c2
@@ -343,14 +363,14 @@
     for i in (1, 2):
         for n in range(3):
             loads[i, n].wait()
-    for n, stage in enumerate((st_o, st_c, st_k)):
-        pack_stage(stage, n)
+    pack_inputs()
     pl.semaphore_wait(barrier, len(greeted))
-    halo = []
-    for n in range(3):
-        halo += edge_copies(n)
-    halo += row_copies(off_m, 0, 0, 5) + row_copies(cnt_m, 1, 0, 5) + row_copies(kap_m, 2, 0, 4)
+    rims = edge_copies(0) + edge_copies(1) + edge_copies(2)
+    start(rims)
+    halo = row_copies(r_m, 0, 0, 5) + row_copies(kap_m, 2, 0, 4) + row_copies(off_m, 1, 0, 3)
     start(halo)
+    rest = row_copies(off_m, 6, 3, 5) + row_copies(kap_m, 5, 4, 6)
+    start(rest)
     load_labels.wait()
 
     def label_copy(k, arriving):
@@ -362,128 +382,144 @@
         label_copy(k, False).start()
     relayout(order[2], False)
     relayout(order[3], False)
+    alive = (left_open, right_open)
+    arrived(rims)
+    e_off = [landed(0, to) for to in range(2)]
+    e_r = [landed(1, to) * alive[to] for to in range(2)]
+    e_kap = [landed(2, to) + 4.0 for to in range(2)]
+    e_w = [10.0 * jnp.exp(v) for v in e_off]
+    for field, edges in ((kap_m, e_kap), (w_m, e_w), (r_m, e_r)):
+        inject(field, edges, TOP, BOTTOM)
+
+    def of_a(r, a):
+        return r * r, r * a, a * a
+
+    def of_b(a, b):
+        return a * b, b * b
+
+    def closed(sums):
+        return [x + y for x, y in zip(*sums)]
+
+    def a_block(q, many, n, sums, counted):
+        shift_block(r_m, a_m, q, many, SHIFTS[0], SIGMA[n], of_a, sums, counted)
+
+    def b_block(q, many, n, sums, counted):
+        shift_block(a_m, b_m, q, many, SHIFTS[1], SIGMA[n], of_b, sums, counted)
+
+    apply_k(r_m, t_m, 9, 39, 6)
+    sums_a = sum_blocks(10, 38, 4, 3, lambda q, sums: a_block(q, 4, 0, sums, range(4)))
+    a_rows = row_copies(a_m, 3, 3, 5)
+    apply_k(a_m, t_m, 11, 35, 4)
+    k_block(a_m, t_m, 35, 2)
+    sums_b = sum_blocks(12, 36, 4, 2, lambda q, sums: b_block(q, 4, 0, sums, range(4)))
+    sums_e = sum_blocks(13, 33, 4, 1, lambda q, sums: energy_block(q, 4, 1.0, sums))
+    energy_block(33, 2, 1.0, sums_e)
+    inject(off_m, e_off, TOP, BOTTOM)
     arrived(halo)
-
-    def halo_rows(do):
-        each(TOP - DEEP, TOP, do)
-        each(BOTTOM, BOTTOM + DEEP, do)
-
-    def prime(q):
+    start(a_rows)
+    for q in (5, 6, 7, 40, 41, 42):
         for p in OWN:
-            weight = jnp.exp(at(off_m, q, p))
-            put(w_m, q, p, 10.0 * weight)
-            put(r_m, q, p, at(cnt_m, q, p) - weight)
-
-    halo_rows(prime)
-    alive = (left_open, right_open)
-    e_off = [landed(0, to) for to in range(2)]
-    e_cnt = [landed(1, to) for to in range(2)]
-    e_kap = [landed(2, to) + 4.0 for to in range(2)]
-    e_w = [jnp.exp(v) for v in e_off]
-    e_r = [(cnt - weight) * live for cnt, weight, live in zip(e_cnt, e_w, alive)]
-    e_w = [10.0 * v for v in e_w]
-    inject(kap_m, e_kap)
-    inject(w_m, e_w)
-    inject(r_m, e_r)
+            put(w_m, q, p, 10.0 * jnp.exp(at(off_m, q, p)))
+    inject_halo(kap_m, e_kap, 0, 4)
+    inject_halo(w_m, e_w)
+    inject_halo(r_m, e_r)
     blank(r_m, TOP - DEEP, BOTTOM + DEEP)
-    for to in range(2):
-        for n, v in enumerate((e_off[to], e_cnt[to], e_w[to], e_r[to])):
-            edge[2 * n + to] = v
-
-    def basis(n):
-        sigma = SIGMA[n]
-        apply_k(r_m, t_m, 4, 44, 4)
-        g00, g01, g11 = shifted(
-            r_m, a_m, 5, 43, 0.0, sigma, lambda q, p, r, a: (r * r, r * a, a * a)
-        )
-        moving = []
-        if n == 0:
-            pack_field(a_m, 3)
-            moving = edge_copies(3) + row_copies(a_m, 3, 3, 5)
-            start(moving)
-        apply_k(a_m, t_m, 6, 42, 4)
-        g12, g22 = shifted(a_m, b_m, 7, 41, SHIFT, sigma, lambda q, p, a, b: (a * b, b * b))
-        if n == 0:
-            pack_field(b_m, 4)
-            more = edge_copies(4) + row_copies(b_m, 4, 1, 5)
-            start(more)
-            moving = moving + more
-
-        def energy(m, carry):
-            carry = list(carry)
-            q = TOP + 4 * m
-            for p in OWN:
-                made, values = k_tile(b_m, q, p, 4)
-                for k in range(4):
-                    square = made[k] * made[k]
-                    carry[k % 2] = carry[k % 2] + (
-                        (square if sigma == 1.0 else sigma * square)
-                        + at(w_m, q + k, p) * (values[k] * values[k])
-                    )
-            return tuple(carry)
-
-        h22 = added(list(lax.fori_loop(0, ROWS // 4, energy, (zero, zero))))
-        moments_out(n, (g00, g01, g11, g12, g22, h22))
-        return moving
-
-    moving = basis(0)
-    moments_on(0)
-
-    arrived(moving)
-    e_a = [landed(3, to) for to in range(2)]
-    e_b = [landed(4, to) for to in range(2)]
-    inject(b_m, [v * live for v, live in zip(e_b, alive)])
-    blank(b_m, TOP - DEEP, BOTTOM + DEEP)
-    apply_k(b_m, t_m, 7, 41, 2)
-
-    def second_k(q):
-        for p in OWN:
-            made, _ = k_tile(t_m, q, p, 4)
-            for m in range(4):
+    k_block(r_m, t_m, 4, 5)
+    k_block(r_m, t_m, 39, 5)
+    blank(t_m, 4, 44)
+    a_block(5, 5, 0, sums_a, (3, 4))
+    a_block(38, 5, 0, sums_a, (0, 1))
+    blank(a_m, 5, 43)
+    k_block(a_m, t_m, 6, 5)
+    k_block(a_m, t_m, 37, 5)
+    blank(t_m, 6, 42)
+    b_block(7, 5, 0, sums_b, (1, 2, 3, 4))
+    b_block(36, 5, 0, sums_b, (0, 1, 2, 3))
+    blank(b_m, 7, 41)
+    b_rows = row_copies(b_m, 4, 1, 7)
+    start(b_rows)
+    energy_block(8, 5, 1.0, sums_e)
+    energy_block(35, 5, 1.0, sums_e)
+    row0 = moments_out(0, closed(sums_a) + closed(sums_b) + closed(sums_e))
+    pack_field(a_m, 3)
+    pack_field(b_m, 4)
+    ab_rims = edge_copies(3) + edge_copies(4)
+    start(ab_rims)
+    moving = a_rows + b_rows + ab_rims
+    arrived(rest)
+    inject_halo(off_m, e_off)
+    inject_halo(kap_m, e_kap, 4, 6)
+    row0 = moments_on(0, row0)
+
+    arrived(ab_rims)
+    inject(a_m, [landed(3, to) for to in range(2)], TOP, BOTTOM)
+    e_b = [landed(4, to) * alive[to] for to in range(2)]
+    inject(b_m, e_b, TOP, BOTTOM)
+    arrived(a_rows)
+    inject_halo(a_m, [landed(3, to) for to in range(2)])
+    arrived(b_rows)
+    inject_halo(b_m, e_b, 0, 7)
+    blank(b_m, 1, 47)
+    apply_k(b_m, t_m, 2, 46, 4)
+    blank(t_m, 2, 46)
+
+    def second_k(q, many):
+        for p in ALL:
+            made, _ = k_tile(t_m, q, p, many)
+            for m in range(many):
                 put(q_m, q + m, p, made[m])
 
-    blocks(TOP, BOTTOM, 4, second_k)
-    pack_field(q_m, 5)
-    final = edge_copies(5) + row_copies(q_m, 5, 0, 5)
-    start(final)
+    blocks(3, 45, 6, lambda q: second_k(q, 6))
     sent(moving)
-
-    c0, c1, c2 = solve(moments_in(0), SIGMA[0])
+    sent(halo)
+
+    c0, c1, c2 = solve(moments_in(0, row0), SIGMA[0])
     d0, d1, d2 = 0.1 * c0, 0.1 * c1, 0.1 * c2
 
-    def renew(off, cnt, weight, r, a, b, qb):
+    def renew(off, weight, r, a, b, qb):
         step = c0 * r + (c1 * a + c2 * b)
-        q_mode = d0 * (a - weight * r) + (d1 * (b + (SHIFT - weight) * a) + d2 * qb)
+        q_mode = d0 * (a + (SHIFTS[0] - weight) * r) + (d1 * (b + (SHIFTS[1] - weight) * a) + d2 * qb)
         fresh = jnp.exp(off + step)
-        return step, (10.0 * SIGMA[1]) * fresh, cnt - fresh - q_mode
-
-    def renew_row(q, keep):
-        for p in OWN:
-            step, fresh, gradient = renew(*(at(f, q, p) for f in (off_m, cnt_m, w_m, r_m, a_m, b_m, q_m)))
-            if keep:
-                put(mode_m, q, p, step)
-            put(w_m, q, p, fresh)
-            put(r_m, q, p, gradient)
-
-    each(TOP, BOTTOM, lambda q: renew_row(q, True))
-    arrived(final)
-    halo_rows(lambda q: renew_row(q, False))
-    e_w, e_r = [], []
-    for to in range(2):
-        _, fresh, gradient = renew(
-            edge[to], edge[2 + to], edge[4 + to], edge[6 + to], e_a[to], e_b[to], landed(5, to)
-        )
-        e_w.append(fresh)
-        e_r.append(gradient * alive[to])
-    inject(w_m, e_w)
-    inject(r_m, e_r)
+        return step, (10.0 * SIGMA[1]) * fresh, ((r + 0.1 * weight) - fresh) - q_mode
+
+    def renew_rows(q, many, keep):
+        for p in range(0, PITCH, 8):
+            for m in range(many):
+                off = at(off_m, q + m, p)
+                weight = at(w_m, q + m, p) if keep else 10.0 * jnp.exp(off)
+                step, fresh, gradient = renew(off, weight, *(at(f, q + m, p) for f in (r_m, a_m, b_m, q_m)))
+                if p == 0:
+                    gradient = jnp.where(lane == 0, jnp.where(sub > 0, gradient, 0.0), gradient)
+                elif p == 72:
+                    gradient = jnp.where(lane == 127, jnp.where(sub < subs - 1, gradient, 0.0), gradient)
+                elif keep:
+                    put(mode_m, q + m, p, step)
+                put(w_m, q + m, p, fresh)
+                put(r_m, q + m, p, gradient)
+
+    blocks(TOP, BOTTOM, 2, lambda q: renew_rows(q, 2, True))
+    each(TOP - DEEP, TOP, lambda q: renew_rows(q, 1, False))
+    each(BOTTOM, BOTTOM + DEEP, lambda q: renew_rows(q, 1, False))
     blank(r_m, TOP - DEEP, BOTTOM + DEEP)
 
-    basis(1)
-    moments_on(1)
-
-    sent(final)
-    sent(halo)
+    apply_k(r_m, t_m, 4, 44, 4)
+    blank(t_m, 4, 44)
+    sums_a = sum_blocks(8, 40, 4, 3, lambda q, sums: a_block(q, 4, 1, sums, range(4)))
+    a_block(5, 3, 1, None, ())
+    a_block(40, 3, 1, None, ())
+    blank(a_m, 5, 43)
+    apply_k(a_m, t_m, 6, 42, 4)
+    blank(t_m, 6, 42)
+    sums_b = sum_blocks(8, 40, 4, 2, lambda q, sums: b_block(q, 4, 1, sums, range(4)))
+    b_block(7, 1, 1, None, ())
+    b_block(40, 1, 1, None, ())
+    blank(b_m, 7, 41)
+    sums_e = sum_blocks(8, 40, 4, 1, lambda q, sums: energy_block(q, 4, SIGMA[1], sums))
+    row1 = moments_out(1, closed(sums_a) + closed(sums_b) + closed(sums_e))
+    row1 = moments_on(1, row1)
+
+    sent(rims)
+    sent(rest)
     for k in range(1, subs):
         label_copy(k, True).wait()
     load_owner.wait()
@@ -498,30 +534,33 @@
         below = below + jnp.where(sublane >= n, pltpu.roll(below, n, axis=0), 0)
     slot = jnp.where(mark == 1, count + below - 1, -1)
     region = (sublane * 128 + lane).astype(F32)
-    tiles = [
-        jnp.concatenate([lab[2 * h], lab[2 * h + 1]], axis=1).astype(F32) for h in range(2)
-    ]
+    tiles = []
+    for h in range(2):
+        pair = jnp.concatenate([lab[2 * h], lab[2 * h + 1]], axis=1).astype(F32)
+        twice = [jnp.broadcast_to(pair[n : n + 1], (2, 128)) for n in range(8)]
+        tiles.append(jnp.concatenate(twice, axis=0))
     for s in range(OWNED_MOST):
         mine = jnp.max(jnp.where(slot == s, region, -1.0), axis=1, keepdims=True)
         mine = jnp.max(mine, axis=0, keepdims=True)
         for h in range(2):
-            pick[s, pl.ds(8 * h, 8), :] = jnp.where(tiles[h] == mine, 1.0, 0.0)
-
-    c0, c1, c2 = solve(moments_in(1), SIGMA[1])
-
-    def finish(q, carry):
-        sums = list(carry)
+            pick[s, h] = jnp.where(tiles[h] == mine, 1.0, 0.0)
+
+    c0, c1, c2 = solve(moments_in(1, row1), SIGMA[1])
+
+    def finish(q, sums):
         for p in OWN:
-            mode = at(mode_m, q, p) + (c0 * at(r_m, q, p) + (c1 * at(a_m, q, p) + c2 * at(b_m, q, p)))
-            put(mode_m, q, p, mode)
-            h = (p // 8) % 4
-            sums[h] = sums[h] + jnp.exp(at(off_m, q, p) + mode)
-        return tuple(sums)
-
-    line = over_sublanes(added(list(lax.fori_loop(TOP, BOTTOM, finish, (zero,) * 4))))
+            for m in range(2):
+                mode = at(mode_m, q + m, p) + (
+                    c0 * at(r_m, q + m, p) + (c1 * at(a_m, q + m, p) + c2 * at(b_m, q + m, p))
+                )
+                put(mode_m, q + m, p, mode)
+                summed(sums, m, [jnp.exp(at(off_m, q + m, p) + mode)])
+
+    line = over_sublanes(closed(sum_blocks(TOP, BOTTOM, 2, 1, finish))[0])
     line = line + pltpu.roll(line, 64, axis=1)
-    mine = (sublane == lax.div(strip, TILE // ROWS)) & (lax.div(lane, 64) == lax.rem(sub, 2))
-    hop1(2, jnp.where(mine, line * (1.0 / (TILE * TILE)), 0.0))
+    mine = lax.div(lane, 64) == lax.rem(sub, 2)
+    row2 = jnp.where(mine, line * (1.0 / (TILE * TILE)), 0.0)[0:1]
+    hop1(2, row2)
 
     outs = []
 
@@ -543,21 +582,18 @@
 
     write_out(0)
     write_out(1)
-    hop_done(peers1, src1, got1, s1, r1, near, 2)
-    both = []
-    for h in range(2):
-        slots = [c * subs + z for c in range(2) for z in (2 * h, 2 * h + 1)]
-        both.append(added([got1[near * 2 + j] for j in slots]))
-    hop2(2, jnp.concatenate(both, axis=0))
+    got = hop1_in(2, row2)
+    upper = lax.div(lax.rem(sublane, subs), 2)
+    rows2 = [over_sublanes(jnp.where(upper == h, got, 0.0))[0:1] for h in range(2)]
+    hop2(2, rows2)
     write_out(2)
     write_out(3)
-    hop_done(peers2, src2, got2, s2, r2, chips, 2)
-    total = added([got2[chips * 2 + j] for j in range(chips)])
+    total = hop2_in(2, rows2)
     answer = zero
     for h in range(2):
         gathered = zero
         for s in range(8 * h, min(8 * h + 8, OWNED_MOST)):
-            both = total * pick[s]
+            both = total[0] * pick[s, 0] + total[1] * pick[s, 1]
             gathered = jnp.where(
                 sublane == s - 8 * h, over_sublanes(both[0:8] + both[8:16]), gathered
             )
@@ -590,18 +626,17 @@
             out_specs=(anywhere, pl.BlockSpec(memory_space=pltpu.VMEM)),
             scratch_shapes=[
                 pltpu.VMEM((2048, 128), jnp.int32), stage, stage,
-                field, field, field, field, field, field, field, field, field, field,
+                field, field, field, field, field, field, field, field, field,
                 pltpu.VMEM((6, 2, 8, 128), F32),
                 pltpu.VMEM((36, 8, 128), F32),
-                pltpu.VMEM((8, 8, 128), F32),
                 pltpu.VMEM((subs, 8, labels.shape[1]), jnp.int32),
                 pltpu.VMEM((8, 128), jnp.int32),
-                pltpu.VMEM((OWNED_MOST, 16, 128), F32),
-                pltpu.VMEM((3, 8, 128), F32),
-                pltpu.VMEM((3, 16, 128), F32),
-                pltpu.VMEM((3 * near, 8, 128), F32),
-                pltpu.VMEM((3 * chips, 16, 128), F32),
-                dma((12,)), dma((2,)), dma((12,)), dma((12,)), dma((36,)), dma((36,)),
+                pltpu.VMEM((OWNED_MOST, 2, chips, 128), F32),
+                pltpu.VMEM((3, 1, 1, 128), F32),
+                pltpu.VMEM((3, 2, 1, 128), F32),
+                pltpu.VMEM((3, 1, near, 128), F32),
+                pltpu.VMEM((3, 2, chips, 128), F32),
+                dma((12,)), dma((2,)), dma((14,)), dma((14,)), dma((36,)), dma((36,)),
                 dma((subs,)), dma((subs,)), dma((3 * near,)), dma((3 * near,)),
                 dma((3 * chips,)), dma((3 * chips,)), dma((4,)),
             ],

time: 60.8 us -> 54.2 us (0.89)
  Pallas kernels: 57.2 us -> 50.6 us
    pallas_call x1, Pallas kernels: 57.2 us -> 50.6 us  [body(): pl.pallas_call(lambda *refs: kernel((strips, subs), *refs), out_shape=(ja...]
where the time goes in v3:
time: 54.2 us; the launch traced here: 54 us
  Pallas kernels  50.6 us (93%)
  local copies, waits for them, and re-layouts  2.78 us (5%)
  between operations  0.65 us (1%)
    pallas_call x1, Pallas kernels, body(): pl.pallas_call(lambda *refs: kernel((strips, subs), *refs), out_shape=(ja...  50.6 us
    unnamed x4, local copies, waits for them, and re-layouts  2.78 us

profile of v3, /device:TPU:0, one launch (start us, length us, event | category | flops | bytes accessed | tf_op | source)
XLA Modules:
  0.0 54.0 jit_solution(16164265367861148040)
XLA Ops:
  0.6 50.6 %shard_map.68 = (f32[2048,128]{1,0:T(8,128)}, f32[1,15]{1,0:T(1,128)}) custom-call(s32[2048,128]{1,0:T(8,128)} %bitcast.22, f32[2048,128]{1,0:T(8,128)} %bitcast.23, f32[2048,128]{1,0:T(8,128)} %bitcast.24, s32[8,64]{1,0:T(8,128)} %refs_3_.1, s32[8,128]{1,0:T(8,128)} %bitcast.26), custom_call_target="tpu_custom_call" | custom-call | tf_op jit(solution)/shard_map/pallas_call | solution.py:619
  51.2 0.0 copy-start
  51.2 2.3 %copy.9 = f32[32,8192]{1,0:T(8,128)} copy(f32[32,8192]{1,0:T(8,128)} %bitcast.25) | data formatting | bytes 2097152
  53.5 0.0 copy-done
  53.5 0.5 copy.10
Async XLA Ops:
  51.2 2.3 %copy-start = (f32[1,15]{1,0:T(1,128)S(1)}, f32[1,15]{1,0:T(1,128)}, u32[]{:S(2)}) copy-start(f32[1,15]{1,0:T(1,128)} %get-tuple-element.5) | copy-start | bytes 184

commit v4 on v3

--- a/solution.py
+++ b/solution.py
@@ -22,37 +22,40 @@
 def kernel(
     dims, counts_h, offset_h, kappa_h, labels_h, owner_h, mode_h, owned_ref,
     st_c, st_o, st_k, off_m, kap_m, w_m, r_m, t_m, a_m, b_m, q_m, mode_m,
-    pack, land, lab, own, pick, src1, src2, got1, got2,
-    ld_sem, small_sem, row_s, row_r, edge_s, edge_r, lab_s, lab_r, s1, r1, s2, r2, out_sem,
+    pack, land, lab, own, pick, src, got,
+    ld_sem, small_sem, row_s, row_r, edge_s, edge_r, lab_s, lab_r, sum_s, sum_r, out_sem,
 ):
     strips, subs = dims
     strip, sub = lax.axis_index("strip"), lax.axis_index("sub")
     core, chip = lax.rem(strip, 2), lax.div(strip, 2)
-    chips, near = strips // 2, 2 * subs
-    me1 = core * subs + sub
+    devices = strips * subs
+    me = sub * strips + strip
     up, down = lax.rem(strip + strips - 1, strips), lax.rem(strip + 1, strips)
     left, right = lax.rem(sub + subs - 1, subs), lax.rem(sub + 1, subs)
     first, last = strip == 0, strip == strips - 1
 
+    side = 4 if strips == 32 else 2
+    tall = strips // 2 // side
+
     def far(n, size):
         return min(n, size - n)
 
-    peers1 = []
-    for flip, dz in sorted(
-        ((f, d) for f in range(2) for d in range(subs) if f or d),
-        key=lambda v: (-far(v[1], subs), -v[0]),
+    def turned_by(x, n, size):
+        return lax.rem(x + n, size) if n else x
+
+    at_y = [turned_by(lax.div(chip, side), n, tall) for n in range(tall)]
+    at_x = [turned_by(lax.rem(chip, side), n, side) for n in range(side)]
+    at_z = [turned_by(sub, n, subs) for n in range(subs)]
+    peers = []
+    for dy, dx, dz, flip in sorted(
+        (
+            (y, x, z, f) for y in range(tall) for x in range(side) for z in range(subs)
+            for f in range(2) if y or x or z or f
+        ),
+        key=lambda v: -far(v[0], tall) - far(v[1], side) - far(v[2], subs),
     ):
-        other, z = (1 - core if flip else core), lax.rem(sub + dz, subs)
-        peers1.append((other * subs + z, (chip * 2 + other, z)))
-    side = 4 if chips == 16 else 2
-    tall = chips // side
-    peers2 = []
-    for dy, dx in sorted(
-        ((y, x) for y in range(tall) for x in range(side) if y or x),
-        key=lambda v: -far(v[0], tall) - far(v[1], side),
-    ):
-        j = lax.rem(lax.div(chip, side) + dy, tall) * side + lax.rem(lax.rem(chip, side) + dx, side)
-        peers2.append((j, (j * 2 + core, sub)))
+        core_ = 1 - core if flip else core
+        peers.append(((at_y[dy] * side + at_x[dx]) * 2 + core_, at_z[dz]))
 
     def each(low, high, do):
         def step(k, carry):
@@ -62,12 +65,7 @@
         lax.fori_loop(low, high, step, 0)
 
     barrier = pltpu.get_barrier_semaphore()
-    around = [
-        (up, sub), (down, sub), (strip, left), (strip, right),
-        (up, left), (down, left), (up, right), (down, right),
-    ]
-    greeted = [device for _, device in peers2 + peers1] + around
-    for device in greeted:
+    for device in peers:
         pl.semaphore_signal(barrier, inc=1, device_id=device, device_id_type=MESH)
 
     order = (0, 3, 1, 2)
@@ -278,31 +276,18 @@
         inject(field, edges, TOP - far_, TOP - near_)
         inject(field, edges, BOTTOM + near_, BOTTOM + far_)
 
-    def hop(peers, src, got, send, recv, size, mine, u):
-        for m, (_, device) in enumerate(peers):
-            remote(src.at[u], got.at[u, :, pl.ds(mine, 1), :], send.at[size * u + m], recv.at[size * u + mine], device).start()
-
-    def hop_done(peers, src, got, send, recv, size, u):
-        for m, (slot, device) in enumerate(peers):
-            remote(src.at[u], got.at[u, :, pl.ds(slot, 1), :], send.at[size * u + m], recv.at[size * u + slot], device).wait()
-
-    def hop1(u, row):
-        src1[u, 0] = row
-        hop(peers1, src1, got1, s1, r1, near, me1, u)
-
-    def hop1_in(u, row):
-        hop_done(peers1, src1, got1, s1, r1, near, u)
-        return jnp.where(sublane[0:near] == me1, row, got1[u, 0])
-
-    def hop2(u, rows):
-        for h in range(2):
-            src2[u, h] = rows[h]
-        hop(peers2, src2, got2, s2, r2, chips, chip, u)
-
-    def hop2_in(u, rows):
-        hop_done(peers2, src2, got2, s2, r2, chips, u)
-        which = lax.broadcasted_iota(jnp.int32, (chips, 128), 0)
-        return [jnp.where(which == chip, rows[h], got2[u, h]) for h in range(2)]
+    def tell(u, row):
+        src[u] = row
+        for device in peers:
+            remote(src.at[u], got.at[u, pl.ds(me, 1), :], sum_s.at[u], sum_r.at[u], device).start()
+
+    def heard(u, row):
+        rows = got.at[u, pl.ds(0, devices - 1), :]
+        remote(rows, rows, sum_s.at[u], sum_r.at[u], peers[0]).wait()
+        made = []
+        for n in range(devices // 8):
+            made.append(jnp.where(sublane + 8 * n == me, row, got[u, pl.ds(8 * n, 8), :]))
+        return made
 
     def added(terms):
         while len(terms) > 1:
@@ -320,16 +305,11 @@
             message = jnp.where(sublane == n, over_sublanes(v), message)
         flat = jnp.sum(message, axis=1, keepdims=True)
         row = over_sublanes(jnp.where(lane == sublane, flat, 0.0))[0:1]
-        hop1(u, row)
+        tell(u, row)
         return row
 
-    def moments_on(u, row):
-        row = over_sublanes(hop1_in(u, row))[0:1]
-        hop2(u, [row, row])
-        return row
-
     def moments_in(u, row):
-        total = over_sublanes(added([v for v in jnp.split(hop2_in(u, [row, row])[0], chips // 8)]))
+        total = over_sublanes(added(heard(u, row)))
         return [jnp.broadcast_to(total[:, n : n + 1], (8, 128)) for n in range(6)]
 
     def solve(moments, sigma):
@@ -364,7 +344,7 @@
         for n in range(3):
             loads[i, n].wait()
     pack_inputs()
-    pl.semaphore_wait(barrier, len(greeted))
+    pl.semaphore_wait(barrier, len(peers))
     rims = edge_copies(0) + edge_copies(1) + edge_copies(2)
     start(rims)
     halo = row_copies(r_m, 0, 0, 5) + row_copies(kap_m, 2, 0, 4) + row_copies(off_m, 1, 0, 3)
@@ -449,7 +429,6 @@
     arrived(rest)
     inject_halo(off_m, e_off)
     inject_halo(kap_m, e_kap, 4, 6)
-    row0 = moments_on(0, row0)
 
     arrived(ab_rims)
     inject(a_m, [landed(3, to) for to in range(2)], TOP, BOTTOM)
@@ -516,7 +495,6 @@
     blank(b_m, 7, 41)
     sums_e = sum_blocks(8, 40, 4, 1, lambda q, sums: energy_block(q, 4, SIGMA[1], sums))
     row1 = moments_out(1, closed(sums_a) + closed(sums_b) + closed(sums_e))
-    row1 = moments_on(1, row1)
 
     sent(rims)
     sent(rest)
@@ -535,15 +513,16 @@
     slot = jnp.where(mark == 1, count + below - 1, -1)
     region = (sublane * 128 + lane).astype(F32)
     tiles = []
-    for h in range(2):
-        pair = jnp.concatenate([lab[2 * h], lab[2 * h + 1]], axis=1).astype(F32)
-        twice = [jnp.broadcast_to(pair[n : n + 1], (2, 128)) for n in range(8)]
-        tiles.append(jnp.concatenate(twice, axis=0))
+    for z in range(subs):
+        wide = jnp.concatenate([lab[z], jnp.full_like(lab[z], -2)], axis=1).astype(F32)
+        for n in range(strips // 8):
+            two = [jnp.broadcast_to(wide[2 * n + k : 2 * n + k + 1], (4, 128)) for k in range(2)]
+            tiles.append(jnp.concatenate(two, axis=0))
     for s in range(OWNED_MOST):
         mine = jnp.max(jnp.where(slot == s, region, -1.0), axis=1, keepdims=True)
         mine = jnp.max(mine, axis=0, keepdims=True)
-        for h in range(2):
-            pick[s, h] = jnp.where(tiles[h] == mine, 1.0, 0.0)
+        for n in range(devices // 8):
+            pick[s, pl.ds(8 * n, 8), :] = jnp.where(tiles[n] == mine, 1.0, 0.0)
 
     c0, c1, c2 = solve(moments_in(1, row1), SIGMA[1])
 
@@ -558,9 +537,8 @@
 
     line = over_sublanes(closed(sum_blocks(TOP, BOTTOM, 2, 1, finish))[0])
     line = line + pltpu.roll(line, 64, axis=1)
-    mine = lax.div(lane, 64) == lax.rem(sub, 2)
-    row2 = jnp.where(mine, line * (1.0 / (TILE * TILE)), 0.0)[0:1]
-    hop1(2, row2)
+    row2 = (line * (1.0 / (TILE * TILE)))[0:1]
+    tell(2, row2)
 
     outs = []
 
@@ -582,20 +560,16 @@
 
     write_out(0)
     write_out(1)
-    got = hop1_in(2, row2)
-    upper = lax.div(lax.rem(sublane, subs), 2)
-    rows2 = [over_sublanes(jnp.where(upper == h, got, 0.0))[0:1] for h in range(2)]
-    hop2(2, rows2)
     write_out(2)
     write_out(3)
-    total = hop2_in(2, rows2)
+    total = heard(2, row2)
     answer = zero
     for h in range(2):
         gathered = zero
         for s in range(8 * h, min(8 * h + 8, OWNED_MOST)):
-            both = total[0] * pick[s, 0] + total[1] * pick[s, 1]
+            both = added([v * pick[s, pl.ds(8 * n, 8), :] for n, v in enumerate(total)])
             gathered = jnp.where(
-                sublane == s - 8 * h, over_sublanes(both[0:8] + both[8:16]), gathered
+                sublane == s - 8 * h, over_sublanes(both), gathered
             )
         flat = jnp.sum(gathered, axis=1, keepdims=True)
         answer = answer + jnp.where(lane == sublane + 8 * h, flat, 0.0)
@@ -606,7 +580,7 @@
 
 def solution(mesh):
     strips, subs = mesh.shape["strip"], mesh.shape["sub"]
-    near, chips = 2 * subs, strips // 2
+    devices = strips * subs
 
     def tiled(x):
         return x.reshape(4, 8, 64, 128).transpose(0, 2, 1, 3).reshape(2048, 128)
@@ -631,17 +605,14 @@
                 pltpu.VMEM((36, 8, 128), F32),
                 pltpu.VMEM((subs, 8, labels.shape[1]), jnp.int32),
                 pltpu.VMEM((8, 128), jnp.int32),
-                pltpu.VMEM((OWNED_MOST, 2, chips, 128), F32),
-                pltpu.VMEM((3, 1, 1, 128), F32),
-                pltpu.VMEM((3, 2, 1, 128), F32),
-                pltpu.VMEM((3, 1, near, 128), F32),
-                pltpu.VMEM((3, 2, chips, 128), F32),
+                pltpu.VMEM((OWNED_MOST, devices, 128), F32),
+                pltpu.VMEM((3, 1, 128), F32),
+                pltpu.VMEM((3, devices, 128), F32),
                 dma((12,)), dma((2,)), dma((14,)), dma((14,)), dma((36,)), dma((36,)),
-                dma((subs,)), dma((subs,)), dma((3 * near,)), dma((3 * near,)),
-                dma((3 * chips,)), dma((3 * chips,)), dma((4,)),
+                dma((subs,)), dma((subs,)), dma((3,)), dma((3,)), dma((4,)),
             ],
             compiler_params=pltpu.CompilerParams(
-                collective_id=0, has_side_effects=True, vmem_limit_bytes=63 << 20
+                collective_id=0, has_side_effects=True, vmem_limit_bytes=55000000
             ),
         )(tiled(counts), tiled(offset), tiled(kappa), labels, owner.reshape(8, 128))
         mode = mode.reshape(4, 64, 8, 128).transpose(0, 2, 1, 3).reshape(32, 8192)

time: 54.2 us -> 49.6 us (0.915); the launches traced: 54 us -> 48.7 us
  Pallas kernels: 50.6 us -> 45.2 us
    pallas_call x1, Pallas kernels: 50.6 us -> 45.2 us  [body(): pl.pallas_call(lambda *refs: kernel((strips, subs), *refs), out_shape=(ja...]
    unnamed x4 -> x6, local copies, waits for them, and re-layouts: 2.78 us -> 2.85 us
where the time goes in v4:
time: 49.6 us; the launch traced here: 48.7 us
  Pallas kernels  45.2 us (91%)
  local copies, waits for them, and re-layouts  2.85 us (6%)
  between operations  0.65 us (1%)
    pallas_call x1, Pallas kernels, body(): pl.pallas_call(lambda *refs: kernel((strips, subs), *refs), out_shape=(ja...  45.2 us
    unnamed x6, local copies, waits for them, and re-layouts  2.85 us

profile of v4, /device:TPU:0, one launch (start us, length us, event | category | flops | bytes accessed | tf_op | source)
XLA Modules:
  0.0 48.7 jit_solution(10620252817205353248)
XLA Ops:
  0.6 0.0 copy-start
  0.6 0.7 %copy-done = s32[8,64]{1,0:T(8,128)S(1)} copy-done((s32[8,64]{1,0:T(8,128)S(1)}, s32[8,64]{1,0:T(8,128)}, u32[]{:S(2)}) %copy-start) | copy-done | bytes 2072
  1.3 0.0 copy-start.1
  1.3 0.7 %copy-done.1 = s32[1024]{0:T(1024)S(1)} copy-done((s32[1024]{0:T(1024)S(1)}, s32[1024]{0:T(1024)}, u32[]{:S(2)}) %copy-start.1) | copy-done | bytes 4120
  2.0 45.2 %shard_map.68 = (f32[2048,128]{1,0:T(8,128)S(1)}, f32[1,15]{1,0:T(1,128)S(1)}) custom-call(s32[2048,128]{1,0:T(8,128)} %bitcast.25, f32[2048,128]{1,0:T(8,128)} %bitcast.26, f32[2048,128]{1,0:T(8,128)} %bitcast.27, s32[8,64]{1,0:T(8,128)S(1)} %copy-done, s32[8,128]{1,0:T(8,128)S(1)} %bitcast.23), custom_call_target="tpu_custom_call" | custom-call | tf_op jit(solution)/shard_map/pallas_call | solution.py:593
  47.2 1.0 %copy.9 = f32[32,8192]{1,0:T(8,128)} copy(f32[32,8192]{1,0:T(8,128)S(1)} %bitcast.22) | data formatting | bytes 2097152
  48.2 0.5 %copy.10 = f32[15]{0:T(128)} copy(f32[15]{0:T(128)S(1)} %bitcast.24) | data formatting | bytes 120
Async XLA Ops:
  0.6 0.7 %copy-start = (s32[8,64]{1,0:T(8,128)S(1)}, s32[8,64]{1,0:T(8,128)}, u32[]{:S(2)}) copy-start(s32[8,64]{1,0:T(8,128)} %refs_3_.1) | copy-start | bytes 6148
  1.3 0.7 %copy-start.1 = (s32[1024]{0:T(1024)S(1)}, s32[1024]{0:T(1024)}, u32[]{:S(2)}) copy-start(s32[1024]{0:T(1024)} %param.9) | copy-start | bytes 12292

commit v5 on v4

--- a/solution.py
+++ b/solution.py
@@ -224,14 +224,14 @@
     def blocks(low, high, many, do):
         each(0, (high - low) // many, lambda n: do(low + many * n))
 
-    def k_block(field, out, q, many):
-        for p in ALL:
+    def k_block(field, out, q, many, tiles=ALL):
+        for p in tiles:
             made, _ = k_tile(field, q, p, many)
             for m in range(many):
                 put(out, q + m, p, made[m])
 
-    def apply_k(field, out, low, high, many):
-        blocks(low, high, many, lambda q: k_block(field, out, q, many))
+    def apply_k(field, out, low, high, many, tiles=ALL):
+        blocks(low, high, many, lambda q: k_block(field, out, q, many, tiles))
 
     def summed(sums, n, terms):
         sums[n % 2] = [x + y for x, y in zip(sums[n % 2], terms)]
@@ -389,14 +389,16 @@
     apply_k(r_m, t_m, 9, 39, 6)
     sums_a = sum_blocks(10, 38, 4, 3, lambda q, sums: a_block(q, 4, 0, sums, range(4)))
     a_rows = row_copies(a_m, 3, 3, 5)
+    start(a_rows)
     apply_k(a_m, t_m, 11, 35, 4)
     k_block(a_m, t_m, 35, 2)
     sums_b = sum_blocks(12, 36, 4, 2, lambda q, sums: b_block(q, 4, 0, sums, range(4)))
+    b_rows = row_copies(b_m, 7, 4, 7)
+    start(b_rows)
     sums_e = sum_blocks(13, 33, 4, 1, lambda q, sums: energy_block(q, 4, 1.0, sums))
     energy_block(33, 2, 1.0, sums_e)
     inject(off_m, e_off, TOP, BOTTOM)
     arrived(halo)
-    start(a_rows)
     for q in (5, 6, 7, 40, 41, 42):
         for p in OWN:
             put(w_m, q, p, 10.0 * jnp.exp(at(off_m, q, p)))
@@ -416,39 +418,45 @@
     b_block(7, 5, 0, sums_b, (1, 2, 3, 4))
     b_block(36, 5, 0, sums_b, (0, 1, 2, 3))
     blank(b_m, 7, 41)
-    b_rows = row_copies(b_m, 4, 1, 7)
-    start(b_rows)
+    outer = row_copies(b_m, 4, 1, 4)
+    start(outer)
+    b_rows = b_rows + outer
     energy_block(8, 5, 1.0, sums_e)
     energy_block(35, 5, 1.0, sums_e)
-    row0 = moments_out(0, closed(sums_a) + closed(sums_b) + closed(sums_e))
     pack_field(a_m, 3)
     pack_field(b_m, 4)
     ab_rims = edge_copies(3) + edge_copies(4)
     start(ab_rims)
+    row0 = moments_out(0, closed(sums_a) + closed(sums_b) + closed(sums_e))
     moving = a_rows + b_rows + ab_rims
     arrived(rest)
     inject_halo(off_m, e_off)
     inject_halo(kap_m, e_kap, 4, 6)
 
+    def second_k(q, many, tiles=ALL):
+        for p in tiles:
+            made, _ = k_tile(t_m, q, p, many)
+            for m in range(many):
+                put(q_m, q + m, p, made[m])
+
+    apply_k(b_m, t_m, 9, 39, 6, OWN)
+    blocks(10, 38, 4, lambda q: second_k(q, 4, OWN[1:-1]))
     arrived(ab_rims)
-    inject(a_m, [landed(3, to) for to in range(2)], TOP, BOTTOM)
     e_b = [landed(4, to) * alive[to] for to in range(2)]
     inject(b_m, e_b, TOP, BOTTOM)
+    apply_k(b_m, t_m, 9, 39, 6, ALL[::9])
+    blocks(10, 38, 4, lambda q: second_k(q, 4, ALL[:2] + ALL[-2:]))
+    inject(a_m, [landed(3, to) for to in range(2)], TOP, BOTTOM)
     arrived(a_rows)
     inject_halo(a_m, [landed(3, to) for to in range(2)])
     arrived(b_rows)
     inject_halo(b_m, e_b, 0, 7)
     blank(b_m, 1, 47)
-    apply_k(b_m, t_m, 2, 46, 4)
+    for q in (2, 39):
+        k_block(b_m, t_m, q, 7)
     blank(t_m, 2, 46)
-
-    def second_k(q, many):
-        for p in ALL:
-            made, _ = k_tile(t_m, q, p, many)
-            for m in range(many):
-                put(q_m, q + m, p, made[m])
-
-    blocks(3, 45, 6, lambda q: second_k(q, 6))
+    for q in (3, 38):
+        second_k(q, 7)
     sent(moving)
     sent(halo)
 
@@ -608,13 +616,13 @@
                 pltpu.VMEM((OWNED_MOST, devices, 128), F32),
                 pltpu.VMEM((3, 1, 128), F32),
                 pltpu.VMEM((3, devices, 128), F32),
-                dma((12,)), dma((2,)), dma((14,)), dma((14,)), dma((36,)), dma((36,)),
+                dma((12,)), dma((2,)), dma((16,)), dma((16,)), dma((36,)), dma((36,)),
                 dma((subs,)), dma((subs,)), dma((3,)), dma((3,)), dma((4,)),
             ],
             compiler_params=pltpu.CompilerParams(
                 collective_id=0, has_side_effects=True, vmem_limit_bytes=55000000
             ),
-        )(tiled(counts), tiled(offset), tiled(kappa), labels, owner.reshape(8, 128))
+        )(tiled(counts), tiled(offset), tiled(kappa), pltpu.with_memory_space_constraint(labels, pltpu.HBM), pltpu.with_memory_space_constraint(owner.reshape(8, 128), pltpu.HBM))
         mode = mode.reshape(4, 64, 8, 128).transpose(0, 2, 1, 3).reshape(32, 8192)
         return mode, owned.reshape(OWNED_MOST)
 

time: 49.6 us -> 47 us (0.948)
  local copies, waits for them, and re-layouts: 2.85 us -> 1.48 us
  Pallas kernels: 45.2 us -> 44 us
    unnamed x6 -> x2, local copies, waits for them, and re-layouts: 2.85 us -> 1.48 us
    pallas_call x1, Pallas kernels: 45.2 us -> 44 us  [body(): pl.pallas_call(lambda *refs: kernel((strips, subs), *refs), out_shape=(ja...]
where the time goes in v5:
time: 47 us; the launch traced here: 46.2 us
  Pallas kernels  44 us (94%)
  local copies, waits for them, and re-layouts  1.48 us (3%)
  between operations  0.64 us (1%)
    pallas_call x1, Pallas kernels, body(): pl.pallas_call(lambda *refs: kernel((strips, subs), *refs), out_shape=(ja...  44 us
    unnamed x2, local copies, waits for them, and re-layouts  1.48 us

profile of v5, /device:TPU:0, one launch (start us, length us, event | category | flops | bytes accessed | tf_op | source)
XLA Modules:
  0.0 46.2 jit_solution(12533818804315484868)
XLA Ops:
  0.6 44.0 %shard_map.68 = (f32[2048,128]{1,0:T(8,128)S(1)}, f32[1,15]{1,0:T(1,128)S(1)}) custom-call(s32[2048,128]{1,0:T(8,128)} %bitcast.24, f32[2048,128]{1,0:T(8,128)} %bitcast.25, f32[2048,128]{1,0:T(8,128)} %bitcast.26, s32[8,64]{1,0:T(8,128)} %refs_3_.1, s32[8,128]{1,0:T(8,128)} %bitcast.27), custom_call_target="tpu_custom_call" | custom-call | tf_op jit(solution)/shard_map/pallas_call | solution.py:601
  44.7 1.0 %copy.9 = f32[32,8192]{1,0:T(8,128)} copy(f32[32,8192]{1,0:T(8,128)S(1)} %bitcast.22) | data formatting | bytes 2097152
  45.7 0.5 %copy.10 = f32[15]{0:T(128)} copy(f32[15]{0:T(128)S(1)} %bitcast.23) | data formatting | bytes 120

commit v6 on v5

--- a/solution.py
+++ b/solution.py
@@ -224,14 +224,14 @@
     def blocks(low, high, many, do):
         each(0, (high - low) // many, lambda n: do(low + many * n))
 
-    def k_block(field, out, q, many, tiles=ALL):
+    def k_block(field, out, q, many, tiles=ALL, scale=1.0):
         for p in tiles:
             made, _ = k_tile(field, q, p, many)
             for m in range(many):
-                put(out, q + m, p, made[m])
-
-    def apply_k(field, out, low, high, many, tiles=ALL):
-        blocks(low, high, many, lambda q: k_block(field, out, q, many, tiles))
+                put(out, q + m, p, made[m] if scale == 1.0 else scale * made[m])
+
+    def apply_k(field, out, low, high, many, tiles=ALL, scale=1.0):
+        blocks(low, high, many, lambda q: k_block(field, out, q, many, tiles, scale))
 
     def summed(sums, n, terms):
         sums[n % 2] = [x + y for x, y in zip(sums[n % 2], terms)]
@@ -241,7 +241,7 @@
             made, _ = k_tile(t_m, q, p, many)
             for m in range(many):
                 value, weight = at(base, q + m, p), at(w_m, q + m, p)
-                got = (made[m] if sigma == 1.0 else sigma * made[m]) + (weight - sigma * shift) * value
+                got = made[m] + (weight - sigma * shift) * value
                 put(out, q + m, p, got)
                 if m in counted and p in OWN:
                     summed(sums, m + p // 8, products(value, got))
@@ -489,13 +489,13 @@
     each(BOTTOM, BOTTOM + DEEP, lambda q: renew_rows(q, 1, False))
     blank(r_m, TOP - DEEP, BOTTOM + DEEP)
 
-    apply_k(r_m, t_m, 4, 44, 4)
+    apply_k(r_m, t_m, 4, 44, 4, ALL, SIGMA[1])
     blank(t_m, 4, 44)
     sums_a = sum_blocks(8, 40, 4, 3, lambda q, sums: a_block(q, 4, 1, sums, range(4)))
     a_block(5, 3, 1, None, ())
     a_block(40, 3, 1, None, ())
     blank(a_m, 5, 43)
-    apply_k(a_m, t_m, 6, 42, 4)
+    apply_k(a_m, t_m, 6, 42, 4, ALL, SIGMA[1])
     blank(t_m, 6, 42)
     sums_b = sum_blocks(8, 40, 4, 2, lambda q, sums: b_block(q, 4, 1, sums, range(4)))
     b_block(7, 1, 1, None, ())
@@ -581,7 +581,7 @@
             )
         flat = jnp.sum(gathered, axis=1, keepdims=True)
         answer = answer + jnp.where(lane == sublane + 8 * h, flat, 0.0)
-    owned_ref[...] = over_sublanes(answer)[0:1, 0:OWNED_MOST]
+    owned_ref[...] = over_sublanes(answer)[0, 0:OWNED_MOST]
     for copy in outs:
         copy.wait()
 
@@ -602,7 +602,7 @@
             lambda *refs: kernel((strips, subs), *refs),
             out_shape=(
                 jax.ShapeDtypeStruct((2048, 128), F32),
-                jax.ShapeDtypeStruct((1, OWNED_MOST), F32),
+                jax.ShapeDtypeStruct((OWNED_MOST,), F32),
             ),
             in_specs=[anywhere] * 5,
             out_specs=(anywhere, pl.BlockSpec(memory_space=pltpu.VMEM)),
@@ -624,7 +624,7 @@
             ),
         )(tiled(counts), tiled(offset), tiled(kappa), pltpu.with_memory_space_constraint(labels, pltpu.HBM), pltpu.with_memory_space_constraint(owner.reshape(8, 128), pltpu.HBM))
         mode = mode.reshape(4, 64, 8, 128).transpose(0, 2, 1, 3).reshape(32, 8192)
-        return mode, owned.reshape(OWNED_MOST)
+        return mode, owned
 
     return jax.shard_map(
         body,

time: 47 us -> 46.9 us (level)
  no operation moved by 1% of the time
where the time goes in v6:
time: 46.9 us; the launch traced here: 46.1 us
  Pallas kernels  44 us (94%)
  local copies, waits for them, and re-layouts  1.48 us (3%)
  between operations  0.64 us (1%)
    pallas_call x1, Pallas kernels, body(): pl.pallas_call(lambda *refs: kernel((strips, subs), *refs), out_shape=(ja...  44 us
    unnamed x2, local copies, waits for them, and re-layouts  1.48 us

profile of v6, /device:TPU:0, one launch (start us, length us, event | category | flops | bytes accessed | tf_op | source)
XLA Modules:
  0.0 46.1 jit_solution(13227528111471881582)
XLA Ops:
  0.6 44.0 %shard_map.68 = (f32[2048,128]{1,0:T(8,128)S(1)}, f32[15]{0:T(128)S(1)}) custom-call(s32[2048,128]{1,0:T(8,128)} %bitcast.22, f32[2048,128]{1,0:T(8,128)} %bitcast.23, f32[2048,128]{1,0:T(8,128)} %bitcast.24, s32[8,64]{1,0:T(8,128)} %refs_3_.1, s32[8,128]{1,0:T(8,128)} %bitcast.25), custom_call_target="tpu_custom_call" | custom-call | tf_op jit(solution)/shard_map/pallas_call | solution.py:601
  44.6 1.0 %copy.9 = f32[32,8192]{1,0:T(8,128)} copy(f32[32,8192]{1,0:T(8,128)S(1)} %bitcast.21) | data formatting | bytes 2097152
  45.6 0.5 %copy.10 = f32[15]{0:T(128)} copy(f32[15]{0:T(128)S(1)} %get-tuple-element.9) | data formatting | bytes 120
